TPU v7x, 256 devices: a whole 4x4x8 slice. The times are simulated.
256 devices in a mesh: ckpt: 16 (over z, core), rows: 16 (over y, x).
Axes of the slice: x: 4, y: 4, z: 8, core: 2. Of those that a mesh axis runs over, the one named last changes fastest.
Arguments:
- deltas: bfloat16 [16, 4096, 14336], P('ckpt', 'rows'), may hold values from -24 to 24
- start_basis: bfloat16 [16, 14336, 64], P('ckpt', 'rows'), may hold values from -6 to 6
- edit_order: int32 [16], replicated, may hold values from 0 to 15, each once
Outputs:
- merged: bfloat16 [4096, 14336], P('rows', 'ckpt')
Inputs may be any that keep to these rules, and one draw needn't show every extreme that they name: `edit_order`: a permutation: each of 0 to 15 appears once.
All inputs are finite; a program needn't handle non-finite values.
Results may differ from a plain program's by a relative error of at most 0.034.
Values may be sent and summed in bfloat16 or wider, within the bound.
A program may use at most 64 MiB of HBM per device.

v0:
```python
import math

import jax
import jax.numpy as jnp
from jax import lax
from jax.sharding import PartitionSpec as P

RANK = 64
SUB_ITERS = 2
NS_ITERS = 4


def broadcast(value, axis, source):
    kept = jnp.where(lax.axis_index(axis) == source, value, 0).astype(value.dtype)
    return lax.psum(kept, axis)


def solve_right(raw, lower_factor):
    return lax.linalg.triangular_solve(
        lower_factor, raw, left_side=False, lower=True, transpose_a=True
    ).astype(jnp.bfloat16)


def local_gram(raw):
    return jnp.dot(raw.T, raw, precision=lax.Precision.HIGHEST)


def cross_gram(stacked, own_cols):
    return lax.dot_general(
        stacked, own_cols, (((0,), (0,)), ((), ())), preferred_element_type=jnp.float32
    )


def update_cols(own_cols, stacked, gram_cols, lead_factor, tail_factor):
    product = jnp.dot(stacked.astype(jnp.float32), gram_cols, precision=lax.Precision.HIGHEST)
    return (lead_factor * own_cols.astype(jnp.float32) + tail_factor * product).astype(jnp.bfloat16)


def body(deltas, start_basis, edit_order):
    changes = deltas[0]
    basis_now = start_basis[0]
    local_rows = changes.shape[0]
    left_basis = jnp.zeros((local_rows, RANK), jnp.bfloat16)
    lower_factor = jnp.zeros((RANK, RANK), jnp.float32)
    for sweep in range(SUB_ITERS):
        left_raw = jnp.dot(
            changes,
            lax.all_gather(basis_now, "rows", axis=0, tiled=True),
            preferred_element_type=jnp.float32,
        )
        left_gram = lax.psum(local_gram(left_raw), "rows")
        left_basis = solve_right(left_raw, jnp.linalg.cholesky(left_gram))
        right_raw = lax.psum_scatter(
            lax.dot_general(
                changes, left_basis, (((0,), (0,)), ((), ())), preferred_element_type=jnp.float32
            ).astype(jnp.bfloat16),
            "rows",
            scatter_dimension=0,
            tiled=True,
        ).astype(jnp.float32)
        right_gram = lax.psum(local_gram(right_raw), "rows")
        lower_factor = jnp.linalg.cholesky(right_gram)
        basis_now = solve_right(right_raw, lower_factor)
    ckpt_count = lax.axis_size("ckpt")
    rows_count = lax.axis_size("rows")
    ckpt_index = lax.axis_index("ckpt")
    left_now = left_basis
    right_now = basis_now
    for step in range(NS_ITERS):
        left_all, right_all = (
            lax.all_gather(left_now, "ckpt", axis=1, tiled=True),
            lax.all_gather(right_now, "ckpt", axis=1, tiled=True),
        )
        gram_left = cross_gram(left_all, left_now)
        gram_right = cross_gram(right_all, right_now)
        gram_left, gram_right = (
            lax.psum(gram_left.astype(jnp.bfloat16), "rows").astype(jnp.float32),
            lax.psum(gram_right.astype(jnp.bfloat16), "rows").astype(jnp.float32),
        )
        if step == 0:
            lead_factor = 1.5 / math.sqrt(ckpt_count)
            tail_factor = -0.5 / (ckpt_count * math.sqrt(ckpt_count))
        else:
            lead_factor = 1.5
            tail_factor = -0.5
        left_now = update_cols(left_now, left_all, gram_left, lead_factor, tail_factor)
        right_now = update_cols(right_now, right_all, gram_right, lead_factor, tail_factor)
    position = jnp.sum(jnp.where(jnp.arange(ckpt_count) == ckpt_index, edit_order, 0))
    weight_now = (1 + position).astype(jnp.float32) / ckpt_count
    scaled_left = jnp.dot(
        left_now.astype(jnp.float32), lower_factor * weight_now, precision=lax.Precision.HIGHEST
    ).astype(jnp.bfloat16)
    left_stack, right_block = (
        lax.all_gather(scaled_left, "ckpt", axis=1, tiled=True),
        lax.all_gather(right_now, "ckpt", axis=1, tiled=True),
    )
    holder = ckpt_index * rows_count // ckpt_count
    right_held = broadcast(right_block, "rows", holder)
    merged = lax.dot_general(
        left_stack, right_held, (((1,), (1,)), ((), ())), preferred_element_type=jnp.float32
    )
    return merged.astype(jnp.bfloat16)


def solution(mesh):
    return jax.shard_map(
        body,
        mesh=mesh,
        in_specs=(P("ckpt", "rows", None), P("ckpt", "rows", None), P()),
        out_specs=P("rows", "ckpt"),
        check_vma=False,
    )
```

profile of v0, /device:TPU:8, one launch (start us, length us, event | category | flops | bytes accessed | tf_op | source)
XLA Modules:
  0.0 1359.9 jit_solution(2458196330878033833)
XLA Ops:
  6.5 0.7 all-gather.21.cloned.1.call-update
  7.3 54.4 %all-gather.21.cloned.1.call-done = bf16[1,14336,64]{1,2,0:T(8,128)(2,1)} async-done(((bf16[1,896,64]{1,2,0:T(8,128)(2,1)}), bf16[1,14336,64]{1,2,0:T(8,128)(2,1)}) %all-gather.21.cloned.1.call-update) | async-done | bytes 1835024 | tf_op jit(solution)/shard_map/all_gather | solution.py:48
  61.7 5.9 fusion.6
  67.9 66.3 %psum.91 = f32[64,64]{0,1:T(8,128)S(1)} all-reduce(f32[64,64]{0,1:T(8,128)S(1)} %fusion.55), channel_id=1, replica_groups=mesh['ckpt'=16,'rows'=16] {'rows'}, use_global_device_ids=true, to_apply=%region_0.0 | all-reduce | flops 4096 | bytes 32768 | tf_op jit(solution)/shard_map/psum | solution.py:51
  134.3 5.8 cholesky.74
  140.8 0.7 fusion.32
  141.5 4.9 custom-call.10
  146.7 4.5 fusion
  151.2 3.0 copy.24
  154.2 84.6 %reduce-scatter.7.cloned.1.call-done = bf16[896,64]{1,0:T(8,128)(2,1)} async-done(((bf16[14336,64]{1,0:T(8,128)(2,1)}), bf16[896,64]{1,0:T(8,128)(2,1)}) %reduce-scatter.7.cloned.1.call-update) | async-done | bytes 114704
  238.8 1.3 fusion.56
  240.1 66.3 %psum.92 = f32[64,64]{0,1:T(8,128)S(1)} all-reduce(f32[64,64]{0,1:T(8,128)S(1)} %fusion.56), channel_id=1, replica_groups=mesh['ckpt'=16,'rows'=16] {'rows'}, use_global_device_ids=true, to_apply=%region_4.7 | all-reduce | flops 4096 | bytes 32768 | tf_op jit(solution)/shard_map/psum | solution.py:61
  306.5 5.8 cholesky.85
  313.0 0.7 fusion.33
  313.7 4.9 custom-call.11
  318.6 1.1 copy.25
  319.6 1.0 fusion.17
  320.8 51.6 %all-gather.9.cloned.1.call-done = bf16[14336,64]{0,1:T(8,128)(2,1)} async-done(((bf16[896,64]{0,1:T(8,128)(2,1)}), bf16[14336,64]{0,1:T(8,128)(2,1)}) %all-gather.9.cloned.1.call-update) | async-done | bytes 1835024 | tf_op jit(solution)/shard_map/all_gather | solution.py:48
  372.4 6.0 fusion.3
  378.6 66.3 %psum.93 = f32[64,64]{0,1:T(8,128)S(1)} all-reduce(f32[64,64]{0,1:T(8,128)S(1)} %fusion.57), channel_id=1, replica_groups=mesh['ckpt'=16,'rows'=16] {'rows'}, use_global_device_ids=true, to_apply=%region_5.9 | all-reduce | flops 4096 | bytes 32768 | tf_op jit(solution)/shard_map/psum | solution.py:51
  445.0 5.8 cholesky.96
  451.5 0.7 fusion.34
  452.2 4.9 custom-call.12
  457.4 4.5 fusion.1
  461.9 3.0 copy.26
  464.9 84.6 %reduce-scatter.9.cloned.1.call-done = bf16[896,64]{1,0:T(8,128)(2,1)} async-done(((bf16[14336,64]{1,0:T(8,128)(2,1)}), bf16[896,64]{1,0:T(8,128)(2,1)}) %reduce-scatter.9.cloned.1.call-update) | async-done | bytes 114704
  549.5 1.3 fusion.58
  550.7 66.3 %psum.98 = f32[64,64]{0,1:T(8,128)S(1)} all-reduce(f32[64,64]{0,1:T(8,128)S(1)} %fusion.58), channel_id=1, replica_groups=mesh['ckpt'=16,'rows'=16] {'rows'}, use_global_device_ids=true, to_apply=%region_11.15 | all-reduce | flops 4096 | bytes 32768 | tf_op jit(solution)/shard_map/psum | solution.py:61
  617.2 5.8 cholesky.107
  623.0 0.7 compare_reduce_fusion
  624.3 4.9 custom-call.13
  629.2 1.1 copy.27
  630.3 1.0 fusion.18
  631.4 41.8 %all-gather.11.cloned.1.call-done = bf16[896,1024]{0,1:T(8,128)(2,1)} async-done(((bf16[896,64]{0,1:T(8,128)(2,1)}), bf16[896,1024]{0,1:T(8,128)(2,1)}) %all-gather.11.cloned.1.call-update) | async-done | bytes 1835024 | tf_op jit(solution)/shard_map/all_gather | solution.py:72
  673.3 3.0 convolution_convert_fusion.6
  676.3 93.3 %all-reduce.10.cloned.1.call-done = bf16[1024,64]{1,0:T(8,128)(2,1)} async-done(((bf16[1024,64]{1,0:T(8,128)(2,1)}), bf16[1024,64]{1,0:T(8,128)(2,1)}) %all-reduce.10.cloned.1.call-update) | async-done | bytes 131088 | tf_op jit(solution)/shard_map/psum | solution.py:78
  769.6 2.0 fusion.13
  771.7 19.2 %all_gather.38 = bf16[256,1024]{0,1:T(8,128)(2,1)S(1)} all-gather(bf16[256,64]{0,1:T(8,128)(2,1)S(1)} %fusion.24), channel_id=1, replica_groups=mesh['ckpt'=16,'rows'=16] {'ckpt'}, dimensions={1}, use_global_device_ids=true | all-gather | bytes 557056 | tf_op jit(solution)/shard_map/all_gather | solution.py:71
  790.9 1.0 convolution_convert_fusion.10
  791.9 19.1 %all-gather.13.cloned.1.call-done = bf16[896,1024]{0,1:T(8,128)(2,1)} async-done(((bf16[896,64]{0,1:T(8,128)(2,1)}), bf16[896,1024]{0,1:T(8,128)(2,1)}) %all-gather.13.cloned.1.call-update) | async-done | bytes 1835024 | tf_op jit(solution)/shard_map/all_gather | solution.py:72
  810.9 3.0 convolution_convert_fusion.5
  814.0 94.1 %all-reduce.18.cloned.1.call-done = (bf16[1024,64]{1,0:T(8,128)(2,1)}, bf16[1024,64]{1,0:T(8,128)(2,1)}) async-done(((bf16[1024,64]{1,0:T(8,128)(2,1)}, bf16[1024,64]{1,0:T(8,128)(2,1)}), (bf16[1024,64]{1,0:T(8,128)(2,1)}, bf16[1024,64]{1,0:T(8,128)(2,1)})) %all-reduce.18.cloned.1.call-update) | async-done | bytes 262160 | tf_op jit(solution)/shard_map/psum | solution.py:77
  908.1 2.1 fusion.14
  910.5 19.1 %all_gather.39 = bf16[256,1024]{0,1:T(8,128)(2,1)S(1)} all-gather(bf16[256,64]{0,1:T(8,128)(2,1)S(1)} %fusion.25), channel_id=1, replica_groups=mesh['ckpt'=16,'rows'=16] {'ckpt'}, dimensions={1}, use_global_device_ids=true | all-gather | bytes 557056 | tf_op jit(solution)/shard_map/all_gather | solution.py:71
  929.7 1.0 convolution_convert_fusion.9
  930.6 19.0 %all-gather.15.cloned.1.call-done = bf16[896,1024]{0,1:T(8,128)(2,1)} async-done(((bf16[896,64]{0,1:T(8,128)(2,1)}), bf16[896,1024]{0,1:T(8,128)(2,1)}) %all-gather.15.cloned.1.call-update) | async-done | bytes 1835024 | tf_op jit(solution)/shard_map/all_gather | solution.py:72
  949.7 3.0 convolution_convert_fusion.4
  952.7 94.0 %all-reduce.16.cloned.1.call-done = (bf16[1024,64]{1,0:T(8,128)(2,1)}, bf16[1024,64]{1,0:T(8,128)(2,1)}) async-done(((bf16[1024,64]{1,0:T(8,128)(2,1)}, bf16[1024,64]{1,0:T(8,128)(2,1)}), (bf16[1024,64]{1,0:T(8,128)(2,1)}, bf16[1024,64]{1,0:T(8,128)(2,1)})) %all-reduce.16.cloned.1.call-update) | async-done | bytes 262160 | tf_op jit(solution)/shard_map/psum | solution.py:77
  1046.7 2.1 fusion.15
  1049.2 19.1 %all_gather.40 = bf16[256,1024]{0,1:T(8,128)(2,1)S(1)} all-gather(bf16[256,64]{0,1:T(8,128)(2,1)S(1)} %fusion.26), channel_id=1, replica_groups=mesh['ckpt'=16,'rows'=16] {'ckpt'}, dimensions={1}, use_global_device_ids=true | all-gather | bytes 557056 | tf_op jit(solution)/shard_map/all_gather | solution.py:71
  1068.3 1.0 convolution_convert_fusion.8
  1069.3 19.0 %all-gather.17.cloned.1.call-done = bf16[896,1024]{0,1:T(8,128)(2,1)} async-done(((bf16[896,64]{0,1:T(8,128)(2,1)}), bf16[896,1024]{0,1:T(8,128)(2,1)}) %all-gather.17.cloned.1.call-update) | async-done | bytes 1835024 | tf_op jit(solution)/shard_map/all_gather | solution.py:72
  1088.3 3.0 convolution_convert_fusion.3
  1091.3 94.0 %all-reduce.14.cloned.1.call-done = (bf16[1024,64]{1,0:T(8,128)(2,1)}, bf16[1024,64]{1,0:T(8,128)(2,1)}) async-done(((bf16[1024,64]{1,0:T(8,128)(2,1)}, bf16[1024,64]{1,0:T(8,128)(2,1)}), (bf16[1024,64]{1,0:T(8,128)(2,1)}, bf16[1024,64]{1,0:T(8,128)(2,1)})) %all-reduce.14.cloned.1.call-update) | async-done | bytes 262160 | tf_op jit(solution)/shard_map/psum | solution.py:77
  1185.3 2.1 fusion.16
  1187.7 19.2 %all_gather.41 = bf16[256,1024]{0,1:T(8,128)(2,1)S(1)} all-gather(bf16[256,64]{0,1:T(8,128)(2,1)S(1)} %fusion.27), channel_id=1, replica_groups=mesh['ckpt'=16,'rows'=16] {'ckpt'}, dimensions={1}, use_global_device_ids=true | all-gather | bytes 557056 | tf_op jit(solution)/shard_map/all_gather | solution.py:71
  1206.9 1.0 convolution_convert_fusion.7
  1207.9 19.0 %all-gather.19.cloned.1.call-done = bf16[896,1024]{0,1:T(8,128)(2,1)} async-done(((bf16[896,64]{0,1:T(8,128)(2,1)}), bf16[896,1024]{0,1:T(8,128)(2,1)}) %all-gather.19.cloned.1.call-update) | async-done | bytes 1835024 | tf_op jit(solution)/shard_map/all_gather | solution.py:95
  1226.8 1.4 broadcast_select_fusion
  1230.1 99.4 %all-reduce.12.cloned.1.call-done = (bf16[1024,64]{1,0:T(8,128)(2,1)}, bf16[896,1024]{0,1:T(8,128)(2,1)}) async-done(((bf16[1024,64]{1,0:T(8,128)(2,1)}, bf16[896,1024]{0,1:T(8,128)(2,1)}), (bf16[1024,64]{1,0:T(8,128)(2,1)}, bf16[896,1024]{0,1:T(8,128)(2,1)})) %all-reduce.12.cloned.1.call-update) | async-done | bytes 1966096 | tf_op jit(solution)/shard_map/psum | solution.py:77
  1329.5 1.2 fusion.28
  1330.7 0.8 convolution_convert_fusion.11
  1331.5 18.9 %all_gather.42 = bf16[256,1024]{0,1:T(8,128)(2,1)S(1)} all-gather(bf16[256,64]{0,1:T(8,128)(2,1)S(1)} %convolution_convert_fusion.11), channel_id=1, replica_groups=mesh['ckpt'=16,'rows'=16] {'ckpt'}, dimensions={1}, use_global_device_ids=true | all-gather | bytes 557056 | tf_op jit(solution)/shard_map/all_gather | solution.py:94
  1350.4 3.0 convolution_convert_fusion.2
  (75 shorter events, 6.8 us)
Async XLA Ops:
  6.5 55.2 %all-gather.21.cloned.1.call-start = ((), (), s32[]{:S(2)}) async-start(), calls=%async_computation.9 | async-start | bytes 1949696 | tf_op jit(solution)/shard_map/all_gather | solution.py:48
  7.3 231.5 %reduce-scatter.7.cloned.1.call-start = ((), (), s32[]{:S(2)}) async-start(), calls=%async_computation.10 | async-start | bytes 3899392
  154.1 218.3 %all-gather.9.cloned.1.call-start = ((), (), s32[]{:S(2)}) async-start(), calls=%async_computation.2 | async-start | bytes 1949696 | tf_op jit(solution)/shard_map/all_gather | solution.py:48
  320.7 228.7 %reduce-scatter.9.cloned.1.call-start = ((), (), s32[]{:S(2)}) async-start(), calls=%async_computation.11 | async-start | bytes 3899392
  464.8 208.4 %all-gather.11.cloned.1.call-start = ((), (), s32[]{:S(2)}) async-start(), calls=%async_computation.3 | async-start | bytes 1949696 | tf_op jit(solution)/shard_map/all_gather | solution.py:72
  631.4 138.2 %copy-start.7 = (bf16[896,64]{0,1:T(8,128)(2,1)S(1)}, bf16[896,64]{0,1:T(8,128)(2,1)}, u32[]{:S(2)}) copy-start(bf16[896,64]{0,1:T(8,128)(2,1)} %fusion.18) | copy-start | bytes 344068
  631.4 138.2 %all-reduce.10.cloned.1.call-start = ((), (), s32[]{:S(2)}) async-start(), calls=%async_computation.4 | async-start | bytes 524288 | tf_op jit(solution)/shard_map/psum | solution.py:78
  673.3 96.3 %copy-start.3 = (bf16[896,1024]{0,1:T(8,128)(2,1)S(1)}, bf16[896,1024]{0,1:T(8,128)(2,1)}, u32[]{:S(2)}) copy-start(bf16[896,1024]{0,1:T(8,128)(2,1)} %all-gather.11.cloned.1.call-done) | copy-start | bytes 5505028
  676.3 134.6 %all-gather.13.cloned.1.call-start = ((), (), s32[]{:S(2)}) async-start(), calls=%async_computation.5 | async-start | bytes 1949696 | tf_op jit(solution)/shard_map/all_gather | solution.py:72
  771.6 136.5 %all-reduce.18.cloned.1.call-start = ((), (), s32[]{:S(2)}) async-start(), calls=%async_computation.15 | async-start | bytes 1048576 | tf_op jit(solution)/shard_map/psum | solution.py:77
  790.9 117.2 %copy-start.6 = (bf16[896,64]{0,1:T(8,128)(2,1)S(1)}, bf16[896,64]{0,1:T(8,128)(2,1)}, u32[]{:S(2)}) copy-start(bf16[896,64]{0,1:T(8,128)(2,1)} %fusion.13) | copy-start | bytes 344068
  810.9 97.2 %copy-start.2 = (bf16[896,1024]{0,1:T(8,128)(2,1)S(1)}, bf16[896,1024]{0,1:T(8,128)(2,1)}, u32[]{:S(2)}) copy-start(bf16[896,1024]{0,1:T(8,128)(2,1)} %all-gather.13.cloned.1.call-done) | copy-start | bytes 5505028
  813.9 135.7 %all-gather.15.cloned.1.call-start = ((), (), s32[]{:S(2)}) async-start(), calls=%async_computation.6 | async-start | bytes 1949696 | tf_op jit(solution)/shard_map/all_gather | solution.py:72
  908.1 2.2 copy-start.9
  910.2 39.5 %copy-start.4 = (bf16[896,64]{0,1:T(8,128)(2,1)S(1)}, bf16[896,64]{0,1:T(8,128)(2,1)}, u32[]{:S(2)}) copy-start(bf16[896,64]{0,1:T(8,128)(2,1)} %fusion.14) | copy-start | bytes 344068
  910.2 136.5 %all-reduce.16.cloned.1.call-start = ((), (), s32[]{:S(2)}) async-start(), calls=%async_computation.14 | async-start | bytes 1048576 | tf_op jit(solution)/shard_map/psum | solution.py:77
  949.7 97.1 %copy-start = (bf16[896,1024]{0,1:T(8,128)(2,1)S(1)}, bf16[896,1024]{0,1:T(8,128)(2,1)}, u32[]{:S(2)}) copy-start(bf16[896,1024]{0,1:T(8,128)(2,1)} %all-gather.15.cloned.1.call-done) | copy-start | bytes 5505028
  952.7 135.6 %all-gather.17.cloned.1.call-start = ((), (), s32[]{:S(2)}) async-start(), calls=%async_computation.7 | async-start | bytes 1949696 | tf_op jit(solution)/shard_map/all_gather | solution.py:72
  1046.7 2.2 copy-start.10
  1048.8 39.5 %copy-start.5 = (bf16[896,64]{0,1:T(8,128)(2,1)S(1)}, bf16[896,64]{0,1:T(8,128)(2,1)}, u32[]{:S(2)}) copy-start(bf16[896,64]{0,1:T(8,128)(2,1)} %fusion.15) | copy-start | bytes 344068
  1048.8 136.5 %all-reduce.14.cloned.1.call-start = ((), (), s32[]{:S(2)}) async-start(), calls=%async_computation.13 | async-start | bytes 1048576 | tf_op jit(solution)/shard_map/psum | solution.py:77
  1088.3 97.0 %copy-start.1 = (bf16[896,1024]{0,1:T(8,128)(2,1)S(1)}, bf16[896,1024]{0,1:T(8,128)(2,1)}, u32[]{:S(2)}) copy-start(bf16[896,1024]{0,1:T(8,128)(2,1)} %all-gather.17.cloned.1.call-done) | copy-start | bytes 5505028
  1091.3 135.6 %all-gather.19.cloned.1.call-start = ((), (), s32[]{:S(2)}) async-start(), calls=%async_computation.8 | async-start | bytes 1949696 | tf_op jit(solution)/shard_map/all_gather | solution.py:95
  1185.3 2.2 copy-start.8
  1187.4 142.1 %all-reduce.12.cloned.1.call-start = ((), (), s32[]{:S(2)}) async-start(), calls=%async_computation.12 | async-start | bytes 4194304 | tf_op jit(solution)/shard_map/psum | solution.py:77
  1228.2 0.7 copy-start.11
Sparse Core Ops, SparseCore 0:
  9.8 51.8 all-gather.20
  154.3 84.4 reduce-scatter.6
  320.8 51.5 all-gather.8
  465.0 84.4 reduce-scatter.8
  631.5 41.7 all-gather.10
  676.4 93.1 all-reduce.9
  771.8 39.1 all-gather.12
  814.2 93.8 all-reduce.17
  910.3 39.2 all-gather.14
  952.8 93.9 all-reduce.15
  1049.0 39.2 all-gather.16
  1091.4 93.8 all-reduce.13
  1187.5 39.2 all-gather.18
  1230.1 99.3 all-reduce.11
where the time goes:
time: 1360 us
  waiting for transfers between devices  869 us (64%)
  blocking collectives  361 us (27%)
  matrix products  56.3 us (4%)
  other arithmetic  50.3 us (4%)
  between operations  14.1 us (1%)
    psum x4, waiting for transfers between devices, body(): lax.psum(gram_left.astype(jnp.bfloat16), 'rows').astype(jnp.float32)  382 us
    unnamed x16, waiting for transfers between devices  170 us
    psum x2, blocking collectives, body(): left_gram = lax.psum(local_gram(left_raw), 'rows')  133 us
    psum x2, blocking collectives, body(): right_gram = lax.psum(local_gram(right_raw), 'rows')  133 us
    all_gather x5, waiting for transfers between devices, body(): lax.all_gather(right_now, 'ckpt', axis=1, tiled=True)  118 us
    all_gather x2, waiting for transfers between devices, body(): lax.all_gather(basis_now, 'rows', axis=0, tiled=True)  106 us
    psum x1, waiting for transfers between devices, body(): lax.psum(gram_right.astype(jnp.bfloat16), 'rows').astype(jnp.float32)  93.3 us
    all_gather x4, blocking collectives, body(): lax.all_gather(left_now, 'ckpt', axis=1, tiled=True)  76.6 us
  transfers between devices with their start and end apart: 14, of which 14 were waited for; matrix products, arithmetic and copies ran while one was open for 0% of the time, Pallas kernels for 0%

commit v1 on v0

v1 whole, which is shorter than its diff:
```python
import jax
import jax.numpy as jnp
from jax import lax
from jax.experimental import pallas as pl
from jax.experimental.pallas import tpu as pltpu
from jax.sharding import PartitionSpec as P

RANK = 64
NS_ITERS = 4
N = 16
COLS = 896
BF = jnp.bfloat16
F32 = jnp.float32
MESH = pl.DeviceIdType.MESH
HIGHEST = lax.Precision.HIGHEST
NT = (((1,), (1,)), ((), ()))


def dot_nt(a, b, precision=None):
    return lax.dot_general(a, b, NT, precision=precision, preferred_element_type=F32)


def factor(gram_wide):
    row = lax.broadcasted_iota(jnp.int32, (RANK, 2 * RANK), 0)
    lane = lax.broadcasted_iota(jnp.int32, (RANK, 2 * RANK), 1)
    work = gram_wide + jnp.where(row == lane, 1.0, 0.0)

    def step(j, w):
        pivot_row = jnp.sum(jnp.where(row == j, w, 0.0), axis=0, keepdims=True)
        column = jnp.sum(jnp.where(lane == j + RANK, w, 0.0), axis=1, keepdims=True)
        pivot = jnp.sum(jnp.where(lane[:1] == j + RANK, pivot_row, 0.0), axis=1, keepdims=True)
        ratio = jnp.where(row[:, :1] > j, column, 0.0) / pivot
        return w - ratio * pivot_row

    work = lax.fori_loop(0, RANK, step, work)
    diagonal = jnp.sum(jnp.where(lane == row + RANK, work, 0.0), axis=1, keepdims=True)
    return work * lax.rsqrt(diagonal)


def subspace_kernel(d_hbm, b_ref, left_ref, right_ref, mid_ref, d, ag, y, rs, g, dsem, ssem, rsem):
    me = lax.axis_index("rows")

    def peer_of(k):
        return lax.rem(me + k, N)

    def copy_to(src, dst, phase, k):
        return pltpu.make_async_remote_copy(
            src_ref=src,
            dst_ref=dst,
            send_sem=ssem.at[phase, k],
            recv_sem=rsem.at[phase, me],
            device_id={"rows": peer_of(k)},
            device_id_type=MESH,
        )

    def arrival(buffer, phase, source):
        pltpu.make_async_remote_copy(
            src_ref=buffer,
            dst_ref=buffer,
            send_sem=ssem.at[phase, 0],
            recv_sem=rsem.at[phase, source],
            device_id={"rows": source},
            device_id_type=MESH,
        ).wait_recv()

    load = pltpu.make_async_copy(d_hbm, d, dsem)
    load.start()

    barrier = pltpu.get_barrier_semaphore()

    @pl.loop(1, N)
    def _(k):
        pl.semaphore_signal(barrier, inc=1, device_id={"rows": peer_of(k)}, device_id_type=MESH)

    pl.semaphore_wait(barrier, N - 1)

    def columns(j):
        return pl.ds(pl.multiple_of(j * COLS, 128), COLS)

    def gather_start(sweep, phase):
        src = b_ref if sweep == 0 else ag.at[1, me]

        @pl.loop(1, N)
        def _(k):
            copy_to(src, ag.at[sweep, me], phase, k).start()

    def left_product(sweep, phase):
        own = b_ref[...] if sweep == 0 else ag[1, me]
        total = dot_nt(own, d[:, columns(me)])

        def step(k, total):
            source = lax.rem(me + N - k, N)
            arrival(ag.at[sweep, source], phase, source)
            return total + dot_nt(ag[sweep, source], d[:, columns(source)])

        return lax.fori_loop(1, N, step, total)

    def gram_start(raw, index, phase):
        wide = jnp.concatenate([jnp.zeros_like(raw), raw], axis=0)
        g[index, me] = dot_nt(raw, wide, HIGHEST)

        @pl.loop(1, N)
        def _(k):
            copy_to(g.at[index, me], g.at[index, me], phase, k).start()

    def gram_factor(index, phase):
        @pl.loop(1, N)
        def _(k):
            source = lax.rem(me + N - k, N)
            arrival(g.at[index, source], phase, source)

        total = g[index, 0]
        for source in range(1, N):
            total = total + g[index, source]
        return factor(total)

    def scatter_start(left16, sweep, phase):
        @pl.loop(1, N)
        def _(k):
            j = peer_of(k)
            y[sweep, j] = jnp.dot(left16, d[:, columns(j)], preferred_element_type=F32).astype(BF)
            copy_to(y.at[sweep, j], rs.at[sweep, me], phase, k).start()

        y[sweep, me] = jnp.dot(left16, d[:, columns(me)], preferred_element_type=F32).astype(BF)

    def scatter_sum(sweep, phase):
        def step(k, total):
            source = lax.rem(me + N - k, N)
            arrival(rs.at[sweep, source], phase, source)
            return total + rs[sweep, source].astype(F32)

        return lax.fori_loop(1, N, step, y[sweep, me].astype(F32))

    gather_start(0, 0)
    load.wait()
    left_raw = left_product(0, 0)
    gram_start(left_raw, 0, 1)
    scatter_start(left_raw.astype(BF), 0, 2)
    left_fact = gram_factor(0, 1)
    right_raw = jnp.dot(left_fact[:, :RANK], scatter_sum(0, 2), precision=HIGHEST)
    gram_start(right_raw, 1, 3)
    ag[1, me] = right_raw.astype(BF)
    gather_start(1, 4)
    right_fact = gram_factor(1, 3)
    left_raw = jnp.dot(right_fact[:, :RANK], left_product(1, 4), precision=HIGHEST)
    gram_start(left_raw, 2, 5)
    scatter_start(left_raw.astype(BF), 1, 6)
    left_fact = gram_factor(2, 5)
    left_ref[...] = jnp.dot(left_fact[:, :RANK], left_raw, precision=HIGHEST).astype(BF)
    right_raw = jnp.dot(left_fact[:, :RANK], scatter_sum(1, 6), precision=HIGHEST)
    gram_start(right_raw, 3, 7)
    right_fact = gram_factor(3, 7)
    mid_ref[...] = right_fact
    right_ref[...] = jnp.dot(right_fact[:, :RANK], right_raw, precision=HIGHEST).astype(BF)

    @pl.loop(1, N)
    def _(k):
        for sweep, phase in ((0, 0), (1, 4)):
            copy_to(ag.at[sweep, me], ag.at[sweep, me], phase, k).wait_send()
        for index, phase in ((0, 1), (1, 3), (2, 5), (3, 7)):
            copy_to(g.at[index, me], g.at[index, me], phase, k).wait_send()
        for sweep, phase in ((0, 2), (1, 6)):
            copy_to(y.at[sweep, me], rs.at[sweep, me], phase, k).wait_send()


def subspace(changes, start_t):
    rows = changes.shape[0]
    vmem = pl.BlockSpec(memory_space=pltpu.VMEM)
    return pl.pallas_call(
        subspace_kernel,
        out_shape=(
            jax.ShapeDtypeStruct((RANK, rows), BF),
            jax.ShapeDtypeStruct((RANK, COLS), BF),
            jax.ShapeDtypeStruct((RANK, 2 * RANK), F32),
        ),
        in_specs=[pl.BlockSpec(memory_space=pl.ANY), vmem],
        out_specs=(vmem, vmem, vmem),
        scratch_shapes=[
            pltpu.VMEM((rows, N * COLS), BF),
            pltpu.VMEM((2, N, RANK, COLS), BF),
            pltpu.VMEM((2, N, RANK, COLS), BF),
            pltpu.VMEM((2, N, RANK, COLS), BF),
            pltpu.VMEM((4, N, RANK, 2 * RANK), F32),
            pltpu.SemaphoreType.DMA,
            pltpu.SemaphoreType.DMA((8, N)),
            pltpu.SemaphoreType.DMA((8, N)),
        ],
        compiler_params=pltpu.CompilerParams(
            collective_id=0, has_side_effects=True, vmem_limit_bytes=40 * 1024 * 1024
        ),
        name="subspace",
    )(changes, start_t)


def whitener(gram):
    def mul(a, b):
        return jnp.dot(a.astype(BF), b.astype(BF), preferred_element_type=F32)

    lead, tail = 1.5 / 4.0, -0.5 / 64.0
    product = lead * jnp.eye(N * RANK, dtype=F32) + tail * gram
    for step in range(NS_ITERS):
        if step > 0:
            lead, tail = 1.5, -0.5
            product = lead * product + tail * mul(product, gram)
        if step < NS_ITERS - 1:
            half = lead * gram + tail * mul(gram, gram)
            gram = lead * half + tail * mul(half, gram)
    return product.astype(BF)


def body(deltas, start_basis, edit_order):
    left_t, right_t, right_fact = subspace(deltas[0], start_basis[0].T)
    ckpt_index = lax.axis_index("ckpt")
    position = jnp.sum(jnp.where(jnp.arange(N) == ckpt_index, edit_order, 0))
    weight = (1 + position).astype(F32) / N
    middle = (right_fact[:, RANK:].T * weight).astype(BF)

    left_all = lax.all_gather(left_t, "ckpt", axis=0, tiled=True)
    swap = [(c * N + r, r * N + c) for c in range(N) for r in range(N)]
    right_swapped = lax.ppermute(right_t, ("ckpt", "rows"), swap)
    right_all = lax.all_gather(right_swapped, "rows", axis=0, tiled=True)
    gram_left = lax.psum(dot_nt(left_all, left_t).astype(BF), "rows")
    gram_right = lax.psum(dot_nt(right_all, right_swapped).astype(BF), "ckpt")
    gram_left = lax.all_gather(gram_left, "ckpt", axis=1, tiled=True).astype(F32)
    gram_right = lax.all_gather(gram_right, "rows", axis=1, tiled=True).astype(F32)
    middles = lax.all_gather(middle, "ckpt", axis=0, tiled=False)
    white_left = whitener(gram_left)
    white_right = whitener(gram_right)
    scaled = jnp.einsum(
        "kcr,crs->kcs", white_left.reshape(N * RANK, N, RANK), middles, preferred_element_type=F32
    ).reshape(N * RANK, N * RANK).astype(BF)
    scaled_left = lax.dot_general(
        left_all, scaled, (((0,), (0,)), ((), ())), preferred_element_type=F32
    ).astype(BF)
    right_white = jnp.dot(white_right, right_all, preferred_element_type=F32).astype(BF)
    return jnp.dot(scaled_left, right_white, preferred_element_type=F32).astype(BF)


def solution(mesh):
    return jax.shard_map(
        body,
        mesh=mesh,
        in_specs=(P("ckpt", "rows", None), P("ckpt", "rows", None), P()),
        out_specs=P("rows", "ckpt"),
        check_vma=False,
    )
```

time: 1360 us -> 573 us (0.42)
  waiting for transfers between devices: 869 us -> 277 us
  blocking collectives: 361 us -> 41.6 us
  Pallas kernels: 0 us -> 143 us
  other arithmetic: 50.3 us -> 0.71 us
  matrix products: 56.3 us -> 82 us
    psum x5 -> x2, waiting for transfers between devices: 475 us -> 185 us  [the longest x1 92.8 us: body(): gram_left = lax.psum(dot_nt(left_all, left_t).astype(BF), 'rows')]
    psum x4 -> x0, blocking collectives: 265 us -> none  [the longest x2 133 us: body(): left_gram = lax.psum(local_gram(left_raw), 'rows')]
    unnamed x16 -> x5, waiting for transfers between devices: 170 us -> 0.08 us
    pallas_call x0 -> x1, Pallas kernels: none -> 143 us  [subspace(): pl.pallas_call(subspace_kernel, out_shape=(jax.ShapeDtypeStruct((RANK, ro...]
    all_gather x7 -> x3, waiting for transfers between devices: 224 us -> 82.8 us  [the longest x1 41.7 us: body(): lax.all_gather(gram_left, 'ckpt', axis=1, tiled=True).astype(F32)]
    all_gather x5 -> x2, blocking collectives: 95.5 us -> 41.6 us  [the longest x1 23.3 us: body(): left_all = lax.all_gather(left_t, 'ckpt', axis=0, tiled=True)]
    another operation x20 -> x0, other arithmetic: 48.3 us -> none  [the longest x8 22.2 us: solve_right(): lax.linalg.triangular_solve(lower_factor, raw, left_side=False, lower=Tru...]
    dot_general x26 -> x21, matrix products: 53.6 us -> 82 us  [the longest x16 71.4 us: mul(): return jnp.dot(a.astype(BF), b.astype(BF), preferred_element_type=F32)]
  transfers between devices with their start and end apart: 14 -> 6, of which waited for: 14 -> 6; matrix products, arithmetic and copies ran while one was open for 0% -> 7% of each run, Pallas kernels for 0% -> 0%
where the time goes in v1:
time: 573 us; the launch traced here: 568 us
  waiting for transfers between devices  277 us (48%)
  Pallas kernels  143 us (25%)
  matrix products  82 us (14%)
  blocking collectives  41.6 us (7%)
  between operations  14.2 us (2%)
    pallas_call x1, Pallas kernels, subspace(): pl.pallas_call(subspace_kernel, out_shape=(jax.ShapeDtypeStruct((RANK, ro...  143 us
    psum x1, waiting for transfers between devices, body(): gram_left = lax.psum(dot_nt(left_all, left_t).astype(BF), 'rows')  92.8 us
    psum x1, waiting for transfers between devices, body(): gram_right = lax.psum(dot_nt(right_all, right_swapped).astype(BF), 'ckpt')  91.7 us
    dot_general x16, matrix products, mul(): return jnp.dot(a.astype(BF), b.astype(BF), preferred_element_type=F32)  71.4 us
    all_gather x1, waiting for transfers between devices, body(): lax.all_gather(gram_left, 'ckpt', axis=1, tiled=True).astype(F32)  41.7 us
    all_gather x1, waiting for transfers between devices, body(): right_all = lax.all_gather(right_swapped, 'rows', axis=0, tiled=True)  27.5 us
    all_gather x1, blocking collectives, body(): left_all = lax.all_gather(left_t, 'ckpt', axis=0, tiled=True)  23.3 us
    all_gather x1, blocking collectives, body(): middles = lax.all_gather(middle, 'ckpt', axis=0, tiled=False)  18.3 us
  transfers between devices with their start and end apart: 6, of which 6 were waited for; matrix products, arithmetic and copies ran while one was open for 7% of the time, Pallas kernels for 0%

profile of v1, /device:TPU:8, one launch (start us, length us, event | category | flops | bytes accessed | tf_op | source)
XLA Modules:
  0.0 568.1 jit_solution(8115946838409532769)
XLA Ops:
  6.5 0.0 all-gather.7.cloned.1.call-start
  6.5 0.0 copy-start
  6.5 3.1 copy-done
  9.6 0.0 copy-start.1
  9.6 0.9 copy-done.1
  10.5 0.0 copy-start.6
  10.5 142.9 %subspace.1 = (bf16[64,256]{1,0:T(8,128)(2,1)S(1)}, bf16[64,896]{1,0:T(8,128)(2,1)S(1)}, f32[64,128]{1,0:T(8,128)S(1)}) custom-call(bf16[256,14336]{1,0:T(8,128)(2,1)S(1)} %bitcast.28, bf16[64,896]{1,0:T(8,128)(2,1)S(1)} %bitcast.29), custom_call_target="tpu_custom_call" | custom-call | tf_op jit(solution)/shard_map/subspace/pallas_call | solution.py:169
  153.4 4.3 collective-permute-start
  157.8 10.0 %collective-permute-done = bf16[64,896]{1,0:T(8,128)(2,1)S(1)} collective-permute-done((bf16[64,896]{1,0:T(8,128)(2,1)S(1)}, bf16[64,896]{1,0:T(8,128)(2,1)S(1)}, u32[]{:S(2)}, u32[]{:S(2)}) %collective-permute-start) | collective-permute-done | bytes 114720 | tf_op jit(solution)/shard_map/ppermute | solution.py:220
  167.8 0.0 copy-start.3
  167.8 0.6 copy-done.3
  168.4 0.0 all-gather.7.cloned.1.call-update
  168.4 0.0 all-reduce.3.cloned.1.call-start
  168.5 23.3 %all_gather.18 = bf16[1024,256]{1,0:T(8,128)(2,1)S(1)} all-gather(bf16[64,256]{1,0:T(8,128)(2,1)S(1)} %get-tuple-element.8), channel_id=1, replica_groups=mesh['ckpt'=16,'rows'=16] {'ckpt'}, dimensions={0}, use_global_device_ids=true | all-gather | bytes 557056 | tf_op jit(solution)/shard_map/all_gather | solution.py:218
  191.8 0.9 convolution_convert_fusion.2
  192.8 0.0 all-reduce.3.cloned.1.call-update
  192.8 0.0 all-reduce.5.cloned.1.call-start
  192.8 27.5 %all-gather.7.cloned.1.call-done = bf16[1024,896]{1,0:T(8,128)(2,1)} async-done(((bf16[64,896]{1,0:T(8,128)(2,1)}), bf16[1024,896]{1,0:T(8,128)(2,1)}) %all-gather.7.cloned.1.call-update) | async-done | bytes 1835024 | tf_op jit(solution)/shard_map/all_gather | solution.py:221
  220.3 2.8 convolution_convert_fusion.3
  223.1 0.0 all-reduce.5.cloned.1.call-update
  223.2 0.0 all-gather.5.cloned.1.call-start
  223.2 92.8 %all-reduce.3.cloned.1.call-done = bf16[1024,64]{0,1:T(8,128)(2,1)} async-done(((bf16[1024,64]{0,1:T(8,128)(2,1)}), bf16[1024,64]{0,1:T(8,128)(2,1)}) %all-reduce.3.cloned.1.call-update) | async-done | bytes 131088 | tf_op jit(solution)/shard_map/psum | solution.py:222
  316.1 0.0 all-gather.5.cloned.1.call-update
  316.1 0.0 all-gather.9.cloned.1.call-start
  316.1 0.0 copy-done.6
  316.2 0.6 fusion.46
  317.4 0.1 fusion.45
  317.5 0.1 copy.30
  317.6 18.3 %all-gather = bf16[1024,64]{1,0:T(8,128)(2,1)S(1)} all-gather(bf16[64,64]{1,0:T(8,128)(2,1)S(1)} %copy.30), channel_id=2, replica_groups=mesh['ckpt'=16,'rows'=16] {'ckpt'}, dimensions={0}, use_global_device_ids=true | all-gather | bytes 139264 | tf_op jit(solution)/shard_map/all_gather | solution.py:226
  335.9 91.7 %all-reduce.5.cloned.1.call-done = bf16[1024,64]{0,1:T(8,128)(2,1)} async-done(((bf16[1024,64]{0,1:T(8,128)(2,1)}), bf16[1024,64]{0,1:T(8,128)(2,1)}) %all-reduce.5.cloned.1.call-update) | async-done | bytes 131088 | tf_op jit(solution)/shard_map/psum | solution.py:223
  427.6 0.0 all-gather.9.cloned.1.call-update
  427.7 41.7 %all-gather.5.cloned.1.call-done = bf16[1024,1024]{0,1:T(8,128)(2,1)} async-done(((bf16[1024,64]{0,1:T(8,128)(2,1)}), bf16[1024,1024]{0,1:T(8,128)(2,1)}) %all-gather.5.cloned.1.call-update) | async-done | bytes 2097168 | tf_op jit(solution)/shard_map/all_gather | solution.py:224
  469.4 0.0 copy-start.4
  469.4 4.7 fusion.75
  474.1 0.0 copy-done.4
  474.1 2.7 multiply_add_fusion.11
  476.8 2.3 multiply_add_fusion.9
  479.2 2.3 multiply_add_fusion.8
  481.5 0.0 copy-start.7
  481.5 4.3 multiply_add_fusion.6
  485.8 2.5 multiply_add_fusion.10
  488.3 0.0 copy-done.7
  488.3 4.7 multiply_add_fusion.7
  493.0 11.5 %add_convert_fusion.2 = bf16[1024,1024]{0,1:T(8,128)(2,1)S(1)} fusion(f32[1024,1024]{0,1:T(8,128)} %multiply_add_fusion.7, f32[1024,1024]{0,1:T(8,128)} %multiply_add_fusion.6, f32[1024,1024]{0,1:T(8,128)} %copy-done.7), kind=kOutput, calls=%fused_computation.16 | convolution fusion | flops 4306501632 | bytes 14680064 | tf_op jit(solution)/shard_map/dot_general | solution.py:197
  504.6 0.8 convolution_convert_fusion
  505.3 0.8 convolution_convert_fusion.1
  506.1 13.6 %all-gather.9.cloned.1.call-done = bf16[1024,1024]{0,1:T(8,128)(2,1)} async-done(((bf16[1024,64]{0,1:T(8,128)(2,1)}), bf16[1024,1024]{0,1:T(8,128)(2,1)}) %all-gather.9.cloned.1.call-update) | async-done | bytes 2097168 | tf_op jit(solution)/shard_map/all_gather | solution.py:225
  519.7 0.0 copy-start.5
  519.7 4.7 fusion.76
  524.4 0.0 copy-done.5
  524.4 2.7 multiply_add_fusion.5
  527.1 2.3 multiply_add_fusion.3
  529.4 2.5 multiply_add_fusion.2
  531.9 0.0 copy-start.8
  532.0 4.3 multiply_add_fusion
  536.3 2.5 multiply_add_fusion.4
  538.7 0.0 copy-done.8
  538.7 4.3 multiply_add_fusion.1
  543.0 0.0 copy-start.2
  543.0 13.0 %add_convert_fusion = bf16[1024,1024]{0,1:T(8,128)(2,1)} fusion(f32[1024,1024]{0,1:T(8,128)} %multiply_add_fusion.1, f32[1024,1024]{0,1:T(8,128)} %multiply_add_fusion, f32[1024,1024]{0,1:T(8,128)} %copy-done.8), kind=kOutput, calls=%fused_computation.8 | convolution fusion | flops 4306501632 | bytes 14680064 | tf_op jit(solution)/shard_map/dot_general | solution.py:197
  556.0 0.0 copy-done.2
  556.1 5.4 fusion.38
Async XLA Ops:
  6.5 213.8 %all-gather.7.cloned.1.call-start = ((), (), s32[]{:S(2)}) async-start(), calls=%async_computation.2 | async-start | bytes 1949696 | tf_op jit(solution)/shard_map/all_gather | solution.py:221
  6.5 3.1 copy-start
  9.6 0.9 copy-start.1
  10.5 305.6 %copy-start.6 = (s32[16]{0:T(128)S(1)}, s32[16]{0:T(128)}, u32[]{:S(2)}) copy-start(s32[16]{0:T(128)} %param.5) | copy-start | bytes 196
  153.4 14.3 %collective-permute-start = (bf16[64,896]{1,0:T(8,128)(2,1)S(1)}, bf16[64,896]{1,0:T(8,128)(2,1)S(1)}, u32[]{:S(2)}, u32[]{:S(2)}) collective-permute-start(bf16[64,896]{1,0:T(8,128)(2,1)S(1)} %get-tuple-element.10), channel_id=1, source_target_pairs={{0,0},{1,16},{2,32},{3,48},{4,64},{5,80},{6,96},{7,112},{8,128},{9... | collective-permute-start | bytes 344072 | tf_op jit(solution)/shard_map/ppermute | solution.py:220
  167.8 0.6 copy-start.3
  168.4 147.6 %all-reduce.3.cloned.1.call-start = ((), (), s32[]{:S(2)}) async-start(), calls=%async_computation | async-start | bytes 262144 | tf_op jit(solution)/shard_map/psum | solution.py:222
  192.8 234.9 %all-reduce.5.cloned.1.call-start = ((), (), s32[]{:S(2)}) async-start(), calls=%async_computation.3 | async-start | bytes 262144 | tf_op jit(solution)/shard_map/psum | solution.py:223
  223.2 246.2 %all-gather.5.cloned.1.call-start = ((), (), s32[]{:S(2)}) async-start(), calls=%async_computation.1 | async-start | bytes 2228224 | tf_op jit(solution)/shard_map/all_gather | solution.py:224
  316.1 203.6 %all-gather.9.cloned.1.call-start = ((), (), s32[]{:S(2)}) async-start(), calls=%async_computation.4 | async-start | bytes 2228224 | tf_op jit(solution)/shard_map/all_gather | solution.py:225
  469.4 4.7 copy-start.4
  481.5 6.8 %copy-start.7 = (f32[1024,1024]{0,1:T(8,128)}, f32[1024,1024]{0,1:T(8,128)S(1)}, u32[]{:S(2)}) copy-start(f32[1024,1024]{0,1:T(8,128)S(1)} %multiply_add_fusion.8) | copy-start | bytes 12582916
  519.7 4.7 copy-start.5
  531.9 6.8 %copy-start.8 = (f32[1024,1024]{0,1:T(8,128)}, f32[1024,1024]{0,1:T(8,128)S(1)}, u32[]{:S(2)}) copy-start(f32[1024,1024]{0,1:T(8,128)S(1)} %multiply_add_fusion.2) | copy-start | bytes 12582916
  543.0 13.0 %copy-start.2 = (bf16[1024,896]{1,0:T(8,128)(2,1)S(1)}, bf16[1024,896]{1,0:T(8,128)(2,1)}, u32[]{:S(2)}) copy-start(bf16[1024,896]{1,0:T(8,128)(2,1)} %all-gather.7.cloned.1.call-done) | copy-start | bytes 5505028
Sparse Core Ops, SparseCore 0:
  168.6 51.7 all-gather.6
  223.5 92.5 all-reduce.2
  318.4 109.2 all-reduce.4
  429.3 40.0 all-gather.4
  471.7 47.9 all-gather.8

commit v2 on v1

--- a/solution.py
+++ b/solution.py
@@ -9,6 +9,9 @@
 NS_ITERS = 4
 N = 16
 COLS = 896
+ROWS = 256
+PACK = ROWS + 2 * RANK
+ALL = N * RANK
 BF = jnp.bfloat16
 F32 = jnp.float32
 MESH = pl.DeviceIdType.MESH
@@ -37,7 +40,7 @@
     return work * lax.rsqrt(diagonal)
 
 
-def subspace_kernel(d_hbm, b_ref, left_ref, right_ref, mid_ref, d, ag, y, rs, g, dsem, ssem, rsem):
+def subspace_kernel(d_hbm, b_ref, pack_ref, right_ref, d, ag, y, rs, g, dsem, ssem, rsem):
     me = lax.axis_index("rows")
 
     def peer_of(k):
@@ -146,11 +149,11 @@
     gram_start(left_raw, 2, 5)
     scatter_start(left_raw.astype(BF), 1, 6)
     left_fact = gram_factor(2, 5)
-    left_ref[...] = jnp.dot(left_fact[:, :RANK], left_raw, precision=HIGHEST).astype(BF)
+    pack_ref[:, :ROWS] = jnp.dot(left_fact[:, :RANK], left_raw, precision=HIGHEST).astype(BF)
     right_raw = jnp.dot(left_fact[:, :RANK], scatter_sum(1, 6), precision=HIGHEST)
     gram_start(right_raw, 3, 7)
     right_fact = gram_factor(3, 7)
-    mid_ref[...] = right_fact
+    pack_ref[:, ROWS:] = right_fact.astype(BF)
     right_ref[...] = jnp.dot(right_fact[:, :RANK], right_raw, precision=HIGHEST).astype(BF)
 
     @pl.loop(1, N)
@@ -169,12 +172,11 @@
     return pl.pallas_call(
         subspace_kernel,
         out_shape=(
-            jax.ShapeDtypeStruct((RANK, rows), BF),
+            jax.ShapeDtypeStruct((RANK, PACK), BF),
             jax.ShapeDtypeStruct((RANK, COLS), BF),
-            jax.ShapeDtypeStruct((RANK, 2 * RANK), F32),
         ),
         in_specs=[pl.BlockSpec(memory_space=pl.ANY), vmem],
-        out_specs=(vmem, vmem, vmem),
+        out_specs=(vmem, vmem),
         scratch_shapes=[
             pltpu.VMEM((rows, N * COLS), BF),
             pltpu.VMEM((2, N, RANK, COLS), BF),
@@ -192,12 +194,275 @@
     )(changes, start_t)
 
 
-def whitener(gram):
+def gather_kernel(pack_ref, right_ref, lall, rall, gram, glp, grp, grs, blk, zst, lsem, ssem, rsem):
+    c = lax.axis_index("ckpt")
+    r = lax.axis_index("rows")
+
+    def rows64(i):
+        return pl.ds(pl.multiple_of(i * RANK, RANK), RANK)
+
+    def rows32(i):
+        return pl.ds(pl.multiple_of(i * 32, 32), 32)
+
+    def tile_of(i):
+        return (
+            pl.ds(pl.multiple_of(lax.rem(i, 2) * 512, 512), 512),
+            pl.ds(pl.multiple_of(lax.div(i, 2) * 128, 128), 128),
+        )
+
+    def send(axis, mine, src, dst, phase, k):
+        return pltpu.make_async_remote_copy(
+            src_ref=src,
+            dst_ref=dst,
+            send_sem=ssem.at[phase, k],
+            recv_sem=rsem.at[phase, mine],
+            device_id={axis: lax.rem(mine + k, N)},
+            device_id_type=MESH,
+        )
+
+    def arrival(axis, buffer, phase, source):
+        pltpu.make_async_remote_copy(
+            src_ref=buffer,
+            dst_ref=buffer,
+            send_sem=ssem.at[phase, 0],
+            recv_sem=rsem.at[phase, source],
+            device_id={axis: source},
+            device_id_type=MESH,
+        ).wait_recv()
+
+    def swap_copy():
+        return pltpu.make_async_remote_copy(
+            src_ref=right_ref,
+            dst_ref=rall.at[rows64(r)],
+            send_sem=ssem.at[7, 0],
+            recv_sem=rsem.at[7, 0],
+            device_id={"ckpt": r, "rows": c},
+            device_id_type=MESH,
+        )
+
+    barrier = pltpu.get_barrier_semaphore()
+
+    @pl.loop(1, N)
+    def _(k):
+        pl.semaphore_signal(barrier, inc=1, device_id={"ckpt": lax.rem(c + k, N)}, device_id_type=MESH)
+        pl.semaphore_signal(barrier, inc=1, device_id={"rows": lax.rem(r + k, N)}, device_id_type=MESH)
+
+    @pl.when(c != r)
+    def _():
+        pl.semaphore_signal(barrier, inc=1, device_id={"ckpt": r, "rows": c}, device_id_type=MESH)
+        pl.semaphore_wait(barrier, 2 * N - 1)
+
+    @pl.when(c == r)
+    def _():
+        pl.semaphore_wait(barrier, 2 * N - 2)
+
+    @pl.when(c != r)
+    def _():
+        pltpu.make_async_remote_copy(
+            src_ref=right_ref,
+            dst_ref=rall.at[rows64(c)],
+            send_sem=ssem.at[7, 0],
+            recv_sem=rsem.at[7, 0],
+            device_id={"ckpt": r, "rows": c},
+            device_id_type=MESH,
+        ).start()
+
+    @pl.loop(1, N)
+    def _(k):
+        send("ckpt", c, pack_ref, lall.at[rows64(c)], 0, k).start()
+
+    own = pltpu.make_async_copy(pack_ref, lall.at[rows64(c)], lsem.at[0])
+    own.start()
+
+    @pl.when(c != r)
+    def _():
+        swap_copy().wait_recv()
+
+    @pl.when(c == r)
+    def _():
+        local = pltpu.make_async_copy(right_ref, rall.at[rows64(r)], lsem.at[1])
+        local.start()
+        local.wait()
+
+    @pl.loop(1, N)
+    def _(k):
+        send("rows", r, rall.at[rows64(r)], rall.at[rows64(r)], 1, k).start()
+
+    own.wait()
+
+    @pl.loop(1, N)
+    def _(k):
+        source = lax.rem(c + N - k, N)
+        arrival("ckpt", lall.at[rows64(source)], 0, source)
+
+    left_all = lall[:, :ROWS]
+    for half in range(2):
+        strip = lall[pl.ds(pl.multiple_of(half * 512 + c * 32, 32), 32), :ROWS]
+        part = dot_nt(strip, left_all).astype(BF)
+        for q in range(8):
+            glp[2 * q + half] = part[:, q * 128 : (q + 1) * 128]
+
+    @pl.loop(1, N)
+    def _(k):
+        send("rows", r, glp.at[lax.rem(r + k, N)], grs.at[0, r], 2, k).start()
+
+    @pl.loop(1, N)
+    def _(k):
+        source = lax.rem(r + N - k, N)
+        arrival("rows", rall.at[rows64(source)], 1, source)
+
+    half_rows, pair = tile_of(r)
+    pair_rows = pl.ds(pl.multiple_of(lax.div(r, 2) * 128, 128), 128)
+    grp[...] = dot_nt(rall[half_rows, :], rall[pair_rows, :]).astype(BF)
+
+    @pl.loop(1, N)
+    def _(k):
+        send("ckpt", c, grp.at[rows32(lax.rem(c + k, N))], grs.at[1, c], 3, k).start()
+
+    def total(axis, mine, side, phase, first):
+        def step(k, value):
+            source = lax.rem(mine + N - k, N)
+            arrival(axis, grs.at[side, source], phase, source)
+            return value + grs[side, source].astype(F32)
+
+        return lax.fori_loop(1, N, step, first.astype(F32)).astype(BF)
+
+    blk[0] = total("rows", r, 0, 2, glp[r])
+    blk[1] = total("ckpt", c, 1, 3, grp[rows32(c)])
+
+    @pl.loop(1, N)
+    def _(k):
+        send("ckpt", c, blk.at[lax.rem(c + k, 2)], zst.at[rows32(c)], 4, k).start()
+
+    zst[rows32(c)] = blk[lax.rem(c, 2)]
+
+    @pl.loop(1, N)
+    def _(k):
+        source = lax.rem(c + N - k, N)
+        arrival("ckpt", zst.at[rows32(source)], 4, source)
+
+    @pl.loop(1, N)
+    def _(k):
+        send("rows", r, zst, gram.at[half_rows, pair], 5, k).start()
+
+    gram[half_rows, pair] = zst[...]
+
+    @pl.loop(1, N)
+    def _(k):
+        source = lax.rem(r + N - k, N)
+        arrival("rows", gram.at[tile_of(source)], 5, source)
+
+    @pl.when(c != r)
+    def _():
+        swap_copy().wait_send()
+
+    @pl.loop(1, N)
+    def _(k):
+        send("ckpt", c, pack_ref, lall.at[rows64(c)], 0, k).wait_send()
+        send("rows", r, rall.at[rows64(r)], rall.at[rows64(r)], 1, k).wait_send()
+        send("rows", r, glp.at[0], grs.at[0, r], 2, k).wait_send()
+        send("ckpt", c, grp.at[rows32(c)], grs.at[1, c], 3, k).wait_send()
+        send("ckpt", c, blk.at[0], zst.at[rows32(c)], 4, k).wait_send()
+        send("rows", r, zst, gram.at[half_rows, pair], 5, k).wait_send()
+
+
+def gather_stacks(pack, right_t):
+    vmem = pl.BlockSpec(memory_space=pltpu.VMEM)
+    return pl.pallas_call(
+        gather_kernel,
+        out_shape=(
+            jax.ShapeDtypeStruct((ALL, PACK), BF),
+            jax.ShapeDtypeStruct((ALL, COLS), BF),
+            jax.ShapeDtypeStruct((ALL, ALL), BF),
+        ),
+        in_specs=[vmem, vmem],
+        out_specs=(vmem, vmem, vmem),
+        scratch_shapes=[
+            pltpu.VMEM((N, 32, 128), BF),
+            pltpu.VMEM((512, 128), BF),
+            pltpu.VMEM((2, N, 32, 128), BF),
+            pltpu.VMEM((2, 32, 128), BF),
+            pltpu.VMEM((512, 128), BF),
+            pltpu.SemaphoreType.DMA((2,)),
+            pltpu.SemaphoreType.DMA((8, N)),
+            pltpu.SemaphoreType.DMA((8, N)),
+        ],
+        compiler_params=pltpu.CompilerParams(
+            collective_id=1, has_side_effects=True, vmem_limit_bytes=40 * 1024 * 1024
+        ),
+        name="gather_stacks",
+    )(pack, right_t)
+
+
+def merge_kernel(own, lall, rall, out, both, scaled, white, lsem, ssem, rsem):
+    c = lax.axis_index("ckpt")
+    side = lax.rem(c, 2)
+    other = c + 1 - 2 * side
+    barrier = pltpu.get_barrier_semaphore()
+    pl.semaphore_signal(barrier, inc=1, device_id={"ckpt": other}, device_id_type=MESH)
+    pl.semaphore_wait(barrier, 1)
+    exchange = pltpu.make_async_remote_copy(
+        src_ref=own,
+        dst_ref=both.at[side],
+        send_sem=ssem,
+        recv_sem=rsem,
+        device_id={"ckpt": other},
+        device_id_type=MESH,
+    )
+    exchange.start()
+    keep = pltpu.make_async_copy(own, both.at[side], lsem)
+    keep.start()
+    keep.wait()
+    pltpu.make_async_remote_copy(
+        src_ref=own,
+        dst_ref=both.at[1 - side],
+        send_sem=ssem,
+        recv_sem=rsem,
+        device_id={"ckpt": other},
+        device_id_type=MESH,
+    ).wait_recv()
+    scaled[...] = lax.dot_general(
+        lall[:, :ROWS], both[0], (((0,), (0,)), ((), ())), preferred_element_type=F32
+    ).astype(BF)
+
+    @pl.loop(0, 4)
+    def _(i):
+        part = pl.ds(pl.multiple_of(i * 256, 256), 256)
+        white[part, :] = jnp.dot(both[1, part, :], rall[...], preferred_element_type=F32).astype(BF)
+
+    out[...] = jnp.dot(scaled[...], white[...], preferred_element_type=F32).astype(BF)
+    exchange.wait_send()
+
+
+def merge(own, lall, rall):
+    vmem = pl.BlockSpec(memory_space=pltpu.VMEM)
+    return pl.pallas_call(
+        merge_kernel,
+        out_shape=jax.ShapeDtypeStruct((ROWS, COLS), BF),
+        in_specs=[vmem, vmem, vmem],
+        out_specs=vmem,
+        scratch_shapes=[
+            pltpu.VMEM((2, ALL, ALL), BF),
+            pltpu.VMEM((ROWS, ALL), BF),
+            pltpu.VMEM((ALL, COLS), BF),
+            pltpu.SemaphoreType.DMA,
+            pltpu.SemaphoreType.DMA,
+            pltpu.SemaphoreType.DMA,
+        ],
+        compiler_params=pltpu.CompilerParams(
+            collective_id=2, has_side_effects=True, vmem_limit_bytes=40 * 1024 * 1024
+        ),
+        name="merge",
+    )(own, lall, rall)
+
+
+def whitener(gram16):
     def mul(a, b):
         return jnp.dot(a.astype(BF), b.astype(BF), preferred_element_type=F32)
 
+    gram = gram16.astype(F32)
     lead, tail = 1.5 / 4.0, -0.5 / 64.0
-    product = lead * jnp.eye(N * RANK, dtype=F32) + tail * gram
+    product = lead * jnp.eye(ALL, dtype=F32) + tail * gram
     for step in range(NS_ITERS):
         if step > 0:
             lead, tail = 1.5, -0.5
@@ -209,31 +474,19 @@
 
 
 def body(deltas, start_basis, edit_order):
-    left_t, right_t, right_fact = subspace(deltas[0], start_basis[0].T)
-    ckpt_index = lax.axis_index("ckpt")
-    position = jnp.sum(jnp.where(jnp.arange(N) == ckpt_index, edit_order, 0))
-    weight = (1 + position).astype(F32) / N
-    middle = (right_fact[:, RANK:].T * weight).astype(BF)
-
-    left_all = lax.all_gather(left_t, "ckpt", axis=0, tiled=True)
-    swap = [(c * N + r, r * N + c) for c in range(N) for r in range(N)]
-    right_swapped = lax.ppermute(right_t, ("ckpt", "rows"), swap)
-    right_all = lax.all_gather(right_swapped, "rows", axis=0, tiled=True)
-    gram_left = lax.psum(dot_nt(left_all, left_t).astype(BF), "rows")
-    gram_right = lax.psum(dot_nt(right_all, right_swapped).astype(BF), "ckpt")
-    gram_left = lax.all_gather(gram_left, "ckpt", axis=1, tiled=True).astype(F32)
-    gram_right = lax.all_gather(gram_right, "rows", axis=1, tiled=True).astype(F32)
-    middles = lax.all_gather(middle, "ckpt", axis=0, tiled=False)
-    white_left = whitener(gram_left)
-    white_right = whitener(gram_right)
-    scaled = jnp.einsum(
-        "kcr,crs->kcs", white_left.reshape(N * RANK, N, RANK), middles, preferred_element_type=F32
-    ).reshape(N * RANK, N * RANK).astype(BF)
-    scaled_left = lax.dot_general(
-        left_all, scaled, (((0,), (0,)), ((), ())), preferred_element_type=F32
+    pack, right_t = subspace(deltas[0], start_basis[0].T)
+    lall, rall, gram = gather_stacks(pack, right_t)
+    white = whitener(gram)
+    weights = jnp.repeat((1 + edit_order).astype(F32) / N, RANK)
+    middle_t = lall[:, ROWS + RANK :].astype(F32) * weights[:, None]
+    block = jnp.arange(ALL) // RANK
+    same = block[:, None] == block[None, :]
+    even = lax.rem(lax.axis_index("ckpt"), 2) == 0
+    scale_t = jnp.where(
+        even, jnp.where(same, jnp.tile(middle_t, (1, N)), 0.0), jnp.eye(ALL, dtype=F32)
     ).astype(BF)
-    right_white = jnp.dot(white_right, right_all, preferred_element_type=F32).astype(BF)
-    return jnp.dot(scaled_left, right_white, preferred_element_type=F32).astype(BF)
+    own = dot_nt(white, scale_t).astype(BF)
+    return merge(own, lall, rall)
 
 
 def solution(mesh):

time: 573 us -> 303 us (0.53)
  waiting for transfers between devices: 277 us -> 0 us
  Pallas kernels: 143 us -> 249 us
  matrix products: 82 us -> 38.9 us
  blocking collectives: 41.6 us -> 0 us
  between operations: 14.2 us -> 0.1 us
  local copies, waits for them, and re-layouts: 4.74 us -> 10.5 us
    psum x2 -> x0, waiting for transfers between devices: 185 us -> none  [the longest x1 92.8 us: body(): gram_left = lax.psum(dot_nt(left_all, left_t).astype(BF), 'rows')]
    pallas_call x1 -> x3, Pallas kernels: 143 us -> 249 us  [the longest x1 143 us: subspace(): pl.pallas_call(subspace_kernel, out_shape=(jax.ShapeDtypeStruct((RANK, PA...]
    all_gather x3 -> x0, waiting for transfers between devices: 82.8 us -> none  [the longest x1 41.7 us: body(): lax.all_gather(gram_left, 'ckpt', axis=1, tiled=True).astype(F32)]
    all_gather x2 -> x0, blocking collectives: 41.6 us -> none  [the longest x1 23.3 us: body(): left_all = lax.all_gather(left_t, 'ckpt', axis=0, tiled=True)]
    dot_general x16 -> x8, matrix products: 71.4 us -> 34.2 us  [mul(): return jnp.dot(a.astype(BF), b.astype(BF), preferred_element_type=F32)]
    ppermute x1 -> x0, waiting for transfers between devices: 9.96 us -> none  [body(): right_swapped = lax.ppermute(right_t, ('ckpt', 'rows'), swap)]
    dot_general x3 -> x0, matrix products: 6.88 us -> none  [the longest x1 5.35 us: body(): jnp.dot(scaled_left, right_white, preferred_element_type=F32).astype(BF)]
  transfers between devices with their start and end apart: 6 -> 0, of which waited for: 6 -> 0; matrix products, arithmetic and copies ran while one was open for 7% -> 0% of each run, Pallas kernels for 0% -> 0%
where the time goes in v2:
time: 303 us; the launch traced here: 299 us
  Pallas kernels  249 us (82%)
  matrix products  38.9 us (13%)
  local copies, waits for them, and re-layouts  10.5 us (3%)
    pallas_call x1, Pallas kernels, subspace(): pl.pallas_call(subspace_kernel, out_shape=(jax.ShapeDtypeStruct((RANK, PA...  143 us
    pallas_call x1, Pallas kernels, gather_stacks(): pl.pallas_call(gather_kernel, out_shape=(jax.ShapeDtypeStruct((ALL, PACK)...  97.5 us
    dot_general x8, matrix products, mul(): return jnp.dot(a.astype(BF), b.astype(BF), preferred_element_type=F32)  34.2 us
    pallas_call x1, Pallas kernels, merge(): pl.pallas_call(merge_kernel, out_shape=jax.ShapeDtypeStruct((ROWS, COLS),...  8.64 us

profile of v2, /device:TPU:8, one launch (start us, length us, event | category | flops | bytes accessed | tf_op | source)
XLA Modules:
  0.0 298.8 jit_solution(14461223251361699409)
XLA Ops:
  0.0 0.0 copy-start
  0.0 3.1 %copy-done = bf16[1,256,14336]{2,1,0:T(8,128)(2,1)S(1)} copy-done((bf16[1,256,14336]{2,1,0:T(8,128)(2,1)S(1)}, bf16[1,256,14336]{2,1,0:T(8,128)(2,1)}, u32[]{:S(2)}) %copy-start) | copy-done | bytes 7340056
  3.1 0.0 copy-start.1
  3.1 0.9 copy-done.1
  4.0 142.9 %subspace.1 = (bf16[64,384]{1,0:T(8,128)(2,1)S(1)}, bf16[64,896]{1,0:T(8,128)(2,1)S(1)}) custom-call(bf16[256,14336]{1,0:T(8,128)(2,1)S(1)} %bitcast.9, bf16[64,896]{1,0:T(8,128)(2,1)S(1)} %bitcast.10), custom_call_target="tpu_custom_call" | custom-call | tf_op jit(solution)/shard_map/subspace/pallas_call | solution.py:172
  146.9 97.5 %gather_stacks.1 = (bf16[1024,384]{1,0:T(8,128)(2,1)S(1)}, bf16[1024,896]{1,0:T(8,128)(2,1)S(1)}, bf16[1024,1024]{1,0:T(8,128)(2,1)S(1)}) custom-call(bf16[64,384]{1,0:T(8,128)(2,1)S(1)} %get-tuple-element.10.pack_ref, bf16[64,896]{1,0:T(8,128)(2,1)S(1)} %get-tuple-element.11.right_ref), custom_call_target="tpu_custom_call" | custom-call | tf_op jit(solution)/shard_map/gather_stacks/pallas_call | solution.py:371
  244.4 2.3 fusion.44
  246.7 2.8 multiply_add_fusion.5
  249.6 2.3 multiply_add_fusion.3
  251.9 2.4 multiply_add_fusion.2
  254.3 0.0 copy-start.3
  254.3 2.5 multiply_add_fusion.4
  256.9 4.3 %multiply_add_fusion.1 = f32[1024,1024]{1,0:T(8,128)} fusion(f32[1024,1024]{1,0:T(8,128)S(1)} %multiply_add_fusion.4, f32[1024,1024]{1,0:T(8,128)S(1)} %multiply_add_fusion.2), kind=kOutput, calls=%fused_computation.8 | convolution fusion | flops 2152726528 | bytes 12582912 | tf_op jit(solution)/shard_map/dot_general | solution.py:461
  261.2 0.0 copy-done.3
  261.2 4.6 %multiply_add_fusion = f32[1024,1024]{1,0:T(8,128)} fusion(f32[1024,1024]{1,0:T(8,128)S(1)} %multiply_add_fusion.2), kind=kOutput, calls=%fused_computation.7 | convolution fusion | flops 2151677952 | bytes 8388608 | tf_op jit(solution)/shard_map/dot_general | solution.py:461
  265.8 0.0 copy-start.2
  265.8 12.9 %add_convert_fusion = bf16[1024,1024]{1,0:T(8,128)(2,1)} fusion(f32[1024,1024]{1,0:T(8,128)} %multiply_add_fusion.1, f32[1024,1024]{1,0:T(8,128)} %multiply_add_fusion, f32[1024,1024]{1,0:T(8,128)} %copy-done.3), kind=kOutput, calls=%fused_computation.5 | convolution fusion | flops 4306501632 | bytes 14680064 | tf_op jit(solution)/shard_map/dot_general | solution.py:461
  278.6 0.0 copy-done.2
  278.6 0.1 broadcast_in_dim.3
  278.7 0.1 mul.90
  278.8 0.3 convert_multiply_fusion.2
  279.1 0.1 copy.6
  279.2 1.6 tile.4
  280.8 3.9 %copy.7 = bf16[1024,1024]{1,0:T(8,128)(2,1)} copy(bf16[1024,1024]{0,1:T(8,128)(2,1)} %bitcast.11) | data formatting | bytes 4194304 | tf_op jit(solution)/shard_map/tile | solution.py:486
  284.7 4.7 %fusion.23.own = bf16[1024,1024]{1,0:T(8,128)(2,1)S(1)} fusion(bf16[1024,1024]{1,0:T(8,128)(2,1)} %add_convert_fusion, bf16[1024,1024]{1,0:T(8,128)(2,1)} %copy.7, s32[1024]{0:T(1024)S(1)} %add_select_fusion, pred[]{:T(512)S(6)} %eq.23), kind=kOutput, calls=%fused_computation.31 | convolution fusion | flops 2153775104 | bytes 6295553 | tf_op jit(solution)/shard_map/dot_general | solution.py:23
  289.4 8.6 %merge.1 = bf16[256,896]{1,0:T(8,128)(2,1)S(1)} custom-call(bf16[1024,1024]{1,0:T(8,128)(2,1)S(1)} %fusion.23.own, bf16[1024,384]{1,0:T(8,128)(2,1)S(1)} %get-tuple-element.13.lall, bf16[1024,896]{1,0:T(8,128)(2,1)S(1)} %get-tuple-element.14.rall), custom_call_target="tpu_custom_call" | custom-call | tf_op jit(solution)/shard_map/merge/pallas_call | solution.py:439
  298.0 0.8 copy.9
  (2 shorter events, 0.0 us)
Async XLA Ops:
  0.0 3.1 %copy-start = (bf16[1,256,14336]{2,1,0:T(8,128)(2,1)S(1)}, bf16[1,256,14336]{2,1,0:T(8,128)(2,1)}, u32[]{:S(2)}) copy-start(bf16[1,256,14336]{2,1,0:T(8,128)(2,1)} %param.3) | copy-start | bytes 22020100
  3.1 0.9 copy-start.1
  254.3 6.9 %copy-start.3 = (f32[1024,1024]{1,0:T(8,128)}, f32[1024,1024]{1,0:T(8,128)S(1)}, u32[]{:S(2)}) copy-start(f32[1024,1024]{1,0:T(8,128)S(1)} %multiply_add_fusion.2) | copy-start | bytes 12582916
  265.8 12.9 %copy-start.2 = (s32[16]{0:T(128)S(1)}, s32[16]{0:T(128)}, u32[]{:S(2)}) copy-start(s32[16]{0:T(128)} %param.5) | copy-start | bytes 196

commit v3 on v2

--- a/solution.py
+++ b/solution.py
@@ -12,6 +12,7 @@
 ROWS = 256
 PACK = ROWS + 2 * RANK
 ALL = N * RANK
+TILE = 256
 BF = jnp.bfloat16
 F32 = jnp.float32
 MESH = pl.DeviceIdType.MESH
@@ -40,130 +41,279 @@
     return work * lax.rsqrt(diagonal)
 
 
-def subspace_kernel(d_hbm, b_ref, pack_ref, right_ref, d, ag, y, rs, g, dsem, ssem, rsem):
-    me = lax.axis_index("rows")
-
-    def peer_of(k):
-        return lax.rem(me + k, N)
-
-    def copy_to(src, dst, phase, k):
+OFFSETS = (0, -1, 1, 2)
+FAR_FIRST = (2, 1, -1, 0)
+
+
+class Plane:
+    def __init__(self, ssem, rsem):
+        self.ssem, self.rsem = ssem, rsem
+        self.r = lax.axis_index("rows")
+        self.x, self.y = lax.rem(self.r, 4), lax.div(self.r, 4)
+        self.sends = []
+
+    def place(self, axis, da, db):
+        dx, dy = (da, db) if axis == 0 else (db, da)
+        return lax.rem(self.y + dy + 4, 4) * 4 + lax.rem(self.x + dx + 4, 4)
+
+    def spot(self, axis, delta):
+        return lax.rem((self.x if axis == 0 else self.y) + delta + 4, 4)
+
+    def copy(self, src, dst, sem, to):
         return pltpu.make_async_remote_copy(
             src_ref=src,
             dst_ref=dst,
-            send_sem=ssem.at[phase, k],
-            recv_sem=rsem.at[phase, me],
-            device_id={"rows": peer_of(k)},
+            send_sem=self.ssem.at[sem],
+            recv_sem=self.rsem.at[sem],
+            device_id={"rows": to},
             device_id_type=MESH,
         )
 
-    def arrival(buffer, phase, source):
-        pltpu.make_async_remote_copy(
-            src_ref=buffer,
-            dst_ref=buffer,
-            send_sem=ssem.at[phase, 0],
-            recv_sem=rsem.at[phase, source],
-            device_id={"rows": source},
-            device_id_type=MESH,
-        ).wait_recv()
-
+    def go(self, src, dst, sem, to):
+        copy = self.copy(src, dst, sem, to)
+        copy.start()
+        self.sends.append(copy)
+
+    def got(self, dst, sem):
+        self.copy(dst, dst, sem, self.r).wait_recv()
+
+    def finish(self):
+        for copy in self.sends:
+            copy.wait_send()
+
+    def gather(self, half, quarter, base, ready):
+        def send(ref, h, slot, da, db):
+            self.go(ref, ref, base + 20 * h + slot, self.place(h, da, db))
+
+        def take(ref, h, slot):
+            self.got(ref, base + 20 * h + slot)
+
+        def spread(h, j):
+            origin = self.place(h, OFFSETS[j], 0)
+            send(half(h, origin), h, 4 + j, 0, 1)
+            send(half(h, origin), h, 8 + j, 0, -1)
+
+        def relay(h, j):
+            origin = self.place(h, OFFSETS[j], -1)
+            take(half(h, origin), h, 4 + j)
+            send(quarter(h, origin, 0), h, 12 + j, 0, 1)
+            origin = self.place(h, OFFSETS[j], 1)
+            take(half(h, origin), h, 8 + j)
+            send(quarter(h, origin, 1), h, 16 + j, 0, -1)
+
+        for h in range(2):
+            send(half(h, self.r), h, 0, 1, 0)
+            send(half(h, self.r), h, 1, -1, 0)
+            spread(h, 0)
+        ready([(0, 0)])
+        for h in range(2):
+            origin = self.place(h, -1, 0)
+            take(half(h, origin), h, 0)
+            send(quarter(h, origin, 0), h, 2, 1, 0)
+            origin = self.place(h, 1, 0)
+            take(half(h, origin), h, 1)
+            send(quarter(h, origin, 1), h, 3, -1, 0)
+        for h in range(2):
+            spread(h, 1)
+            spread(h, 2)
+        for h in range(2):
+            relay(h, 0)
+        for h in range(2):
+            origin = self.place(h, 2, 0)
+            take(quarter(h, origin, 0), h, 2)
+            take(quarter(h, origin, 1), h, 3)
+            spread(h, 3)
+        ready([(-1, 0), (1, 0), (0, -1), (0, 1)])
+        for j in (1, 2):
+            for h in range(2):
+                relay(h, j)
+        ready([(-1, -1), (1, -1), (-1, 1), (1, 1)])
+        for h in range(2):
+            relay(h, 3)
+        groups = ([(0, 2), (2, 0)], [(-1, 2), (2, -1)], [(1, 2), (2, 1)], [(2, 2)])
+        for j in range(4):
+            for h in range(2):
+                origin = self.place(h, OFFSETS[j], 2)
+                take(quarter(h, origin, 0), h, 12 + j)
+                take(quarter(h, origin, 1), h, 16 + j)
+            ready(groups[j])
+
+    def scatter(self, part, y, t1, t2, s1, u1, u2, base, between):
+        done = set()
+
+        def make(dx, dy):
+            if (dx, dy) in done:
+                return
+            done.add((dx, dy))
+            xs, ys = self.spot(0, dx), self.spot(1, dy)
+            value = part(ys * 4 + xs).astype(BF)
+            y[0, ys, xs] = value[:32]
+            y[1, xs, ys] = value[32:]
+
+        def low(q):
+            return pl.ds(16 * q, 16)
+
+        for i, j in enumerate(FAR_FIRST):
+            for h in range(2):
+                make(*((j, 2) if h == 0 else (2, j)))
+                b, a = self.spot(1 - h, 2), self.spot(h, j)
+                for q in range(2):
+                    self.go(
+                        y.at[h, b, a, low(q)], t1.at[h, q, i], base + 20 * h + 4 * q + i,
+                        self.place(h, 0, 1 - 2 * q),
+                    )
+        between()
+        for i, j in enumerate(FAR_FIRST):
+            for h in range(2):
+                for q in range(2):
+                    delta = 1 - 2 * q
+                    make(*((j, delta) if h == 0 else (delta, j)))
+                    b, a = self.spot(1 - h, delta), self.spot(h, j)
+                    self.got(t1.at[h, q, i], base + 20 * h + 4 * q + i)
+                    y[h, b, a, low(q)] = (
+                        y[h, b, a, low(q)].astype(F32) + t1[h, q, i].astype(F32)
+                    ).astype(BF)
+                    self.go(
+                        y.at[h, b, a], t2.at[h, q, i], base + 20 * h + 8 + 4 * q + i,
+                        self.place(h, 0, delta),
+                    )
+        make(0, 0)
+        result = [None, None]
+        for i, j in enumerate(FAR_FIRST):
+            for h in range(2):
+                b, a = self.spot(1 - h, 0), self.spot(h, j)
+                make(*((j, 0) if h == 0 else (0, j)))
+                self.got(t2.at[h, 0, i], base + 20 * h + 8 + i)
+                self.got(t2.at[h, 1, i], base + 20 * h + 12 + i)
+                total = y[h, b, a].astype(F32) + t2[h, 0, i].astype(F32) + t2[h, 1, i].astype(F32)
+                if j == 2:
+                    s1[h, i] = total.astype(BF)
+                    for q in range(2):
+                        self.go(
+                            s1.at[h, i, low(q)], u1.at[h, q], base + 20 * h + 16 + q,
+                            self.place(h, 1 - 2 * q, 0),
+                        )
+                elif j != 0:
+                    q = 0 if j == 1 else 1
+                    self.got(u1.at[h, q], base + 20 * h + 16 + q)
+                    s1[h, i] = total.astype(BF)
+                    s1[h, i, low(q)] = (
+                        total[16 * q : 16 * q + 16] + u1[h, q].astype(F32)
+                    ).astype(BF)
+                    self.go(
+                        s1.at[h, i], u2.at[h, q], base + 20 * h + 18 + q, self.place(h, j, 0)
+                    )
+                else:
+                    result[h] = total
+        for h in range(2):
+            for q in range(2):
+                self.got(u2.at[h, q], base + 20 * h + 18 + q)
+                result[h] = result[h] + u2[h, q].astype(F32)
+        return jnp.concatenate(result, axis=0)
+
+
+def subspace_kernel(
+    d_hbm, b_ref, pack_ref, right_ref, d, ag, y, t1, t2, s1, u1, u2, gx, gy, dsem, ssem, rsem
+):
+    plane = Plane(ssem, rsem)
+    me = plane.r
     load = pltpu.make_async_copy(d_hbm, d, dsem)
     load.start()
-
     barrier = pltpu.get_barrier_semaphore()
 
     @pl.loop(1, N)
     def _(k):
-        pl.semaphore_signal(barrier, inc=1, device_id={"rows": peer_of(k)}, device_id_type=MESH)
-
+        pl.semaphore_signal(barrier, inc=1, device_id={"rows": lax.rem(me + k, N)}, device_id_type=MESH)
+
+    ag[0, me] = b_ref[...]
     pl.semaphore_wait(barrier, N - 1)
 
     def columns(j):
         return pl.ds(pl.multiple_of(j * COLS, 128), COLS)
 
-    def gather_start(sweep, phase):
-        src = b_ref if sweep == 0 else ag.at[1, me]
-
-        @pl.loop(1, N)
-        def _(k):
-            copy_to(src, ag.at[sweep, me], phase, k).start()
-
-    def left_product(sweep, phase):
-        own = b_ref[...] if sweep == 0 else ag[1, me]
-        total = dot_nt(own, d[:, columns(me)])
-
-        def step(k, total):
-            source = lax.rem(me + N - k, N)
-            arrival(ag.at[sweep, source], phase, source)
-            return total + dot_nt(ag[sweep, source], d[:, columns(source)])
-
-        return lax.fori_loop(1, N, step, total)
-
-    def gram_start(raw, index, phase):
-        wide = jnp.concatenate([jnp.zeros_like(raw), raw], axis=0)
-        g[index, me] = dot_nt(raw, wide, HIGHEST)
-
-        @pl.loop(1, N)
-        def _(k):
-            copy_to(g.at[index, me], g.at[index, me], phase, k).start()
-
-    def gram_factor(index, phase):
-        @pl.loop(1, N)
-        def _(k):
-            source = lax.rem(me + N - k, N)
-            arrival(g.at[index, source], phase, source)
-
-        total = g[index, 0]
-        for source in range(1, N):
-            total = total + g[index, source]
-        return factor(total)
-
-    def scatter_start(left16, sweep, phase):
-        @pl.loop(1, N)
-        def _(k):
-            j = peer_of(k)
-            y[sweep, j] = jnp.dot(left16, d[:, columns(j)], preferred_element_type=F32).astype(BF)
-            copy_to(y.at[sweep, j], rs.at[sweep, me], phase, k).start()
-
-        y[sweep, me] = jnp.dot(left16, d[:, columns(me)], preferred_element_type=F32).astype(BF)
-
-    def scatter_sum(sweep, phase):
-        def step(k, total):
-            source = lax.rem(me + N - k, N)
-            arrival(rs.at[sweep, source], phase, source)
-            return total + rs[sweep, source].astype(F32)
-
-        return lax.fori_loop(1, N, step, y[sweep, me].astype(F32))
-
-    gather_start(0, 0)
-    load.wait()
-    left_raw = left_product(0, 0)
-    gram_start(left_raw, 0, 1)
-    scatter_start(left_raw.astype(BF), 0, 2)
-    left_fact = gram_factor(0, 1)
-    right_raw = jnp.dot(left_fact[:, :RANK], scatter_sum(0, 2), precision=HIGHEST)
-    gram_start(right_raw, 1, 3)
+    def left_product(sweep, base, between):
+        total = [jnp.zeros((RANK, ROWS), F32)]
+
+        def ready(sources):
+            for dx, dy in sources:
+                source = plane.place(0, dx, dy)
+                if (dx, dy) == (0, 0) and sweep == 0:
+                    load.wait()
+                total[0] = total[0] + dot_nt(ag[sweep, source], d[:, columns(source)])
+            if len(sources) == 4 and sources[0] == (-1, 0):
+                between()
+
+        plane.gather(
+            lambda h, o: ag.at[sweep, o, pl.ds(32 * h, 32)],
+            lambda h, o, q: ag.at[sweep, o, pl.ds(32 * h + 16 * q, 16)],
+            base,
+            ready,
+        )
+        return total[0]
+
+    def right_product(left16, sweep, base, between):
+        return plane.scatter(
+            lambda j: jnp.dot(left16, d[:, columns(j)], preferred_element_type=F32),
+            *(ref.at[sweep] for ref in (y, t1, t2, s1, u1, u2)),
+            base,
+            between,
+        )
+
+    def exchange(buffer, axis, base):
+        mine = plane.spot(axis, 0)
+        for k in range(1, 4):
+            plane.go(buffer.at[mine], buffer.at[mine], base + k, plane.place(axis, k, 0))
+
+    def collect(buffer, axis, base):
+        for k in range(1, 4):
+            plane.got(buffer.at[plane.spot(axis, -k)], base + k)
+        return (buffer[0] + buffer[1]) + (buffer[2] + buffer[3])
+
+    def gram_start(raw, index):
+        wide = dot_nt(raw, jnp.concatenate([jnp.zeros_like(raw), raw], axis=0), HIGHEST)
+        gx[index, plane.x] = pltpu.roll(wide[:32], RANK, 1) + wide[32:]
+        exchange(gx.at[index], 0, 160 + 8 * index)
+
+    def gram_middle(index):
+        gy[index, plane.y] = collect(gx.at[index], 0, 160 + 8 * index)
+        exchange(gy.at[index], 1, 164 + 8 * index)
+
+    def gram_factor(index):
+        total = collect(gy.at[index], 1, 164 + 8 * index)
+        right = lax.broadcasted_iota(jnp.int32, (32, 128), 1) >= RANK
+        upper = jnp.where(right, pltpu.roll(total, RANK, 1), 0.0)
+        lower = jnp.where(right, total, 0.0)
+        return factor(jnp.concatenate([upper, lower], axis=0))
+
+    left_raw = left_product(0, 0, lambda: None)
+    gram_start(left_raw, 0)
+    facts = {}
+
+    def left_between(index):
+        gram_middle(index)
+        facts[index] = gram_factor(index)
+
+    right_sum = right_product(left_raw.astype(BF), 0, 80, lambda: left_between(0))
+    right_raw = jnp.dot(facts[0][:, :RANK], right_sum, precision=HIGHEST)
     ag[1, me] = right_raw.astype(BF)
-    gather_start(1, 4)
-    right_fact = gram_factor(1, 3)
-    left_raw = jnp.dot(right_fact[:, :RANK], left_product(1, 4), precision=HIGHEST)
-    gram_start(left_raw, 2, 5)
-    scatter_start(left_raw.astype(BF), 1, 6)
-    left_fact = gram_factor(2, 5)
-    pack_ref[:, :ROWS] = jnp.dot(left_fact[:, :RANK], left_raw, precision=HIGHEST).astype(BF)
-    right_raw = jnp.dot(left_fact[:, :RANK], scatter_sum(1, 6), precision=HIGHEST)
-    gram_start(right_raw, 3, 7)
-    right_fact = gram_factor(3, 7)
-    pack_ref[:, ROWS:] = right_fact.astype(BF)
+
+    def right_between(index):
+        gram_middle(index)
+        facts[index] = gram_factor(index)
+
+    gram_start(right_raw, 1)
+    left_product_1 = left_product(1, 40, lambda: right_between(1))
+    left_raw = jnp.dot(facts[1][:, :RANK], left_product_1, precision=HIGHEST)
+    gram_start(left_raw, 2)
+    right_sum = right_product(left_raw.astype(BF), 1, 120, lambda: left_between(2))
+    right_raw = jnp.dot(facts[2][:, :RANK], right_sum, precision=HIGHEST)
+    gram_start(right_raw, 3)
+    pack_ref[:, :ROWS] = jnp.dot(facts[2][:, :RANK], left_raw, precision=HIGHEST).astype(BF)
+    gram_middle(3)
+    right_fact = gram_factor(3)
+    pack_ref[:, ROWS:] = pltpu.roll(right_fact, RANK, 1).astype(BF)
     right_ref[...] = jnp.dot(right_fact[:, :RANK], right_raw, precision=HIGHEST).astype(BF)
-
-    @pl.loop(1, N)
-    def _(k):
-        for sweep, phase in ((0, 0), (1, 4)):
-            copy_to(ag.at[sweep, me], ag.at[sweep, me], phase, k).wait_send()
-        for index, phase in ((0, 1), (1, 3), (2, 5), (3, 7)):
-            copy_to(g.at[index, me], g.at[index, me], phase, k).wait_send()
-        for sweep, phase in ((0, 2), (1, 6)):
-            copy_to(y.at[sweep, me], rs.at[sweep, me], phase, k).wait_send()
+    plane.finish()
 
 
 def subspace(changes, start_t):
@@ -180,15 +330,20 @@
         scratch_shapes=[
             pltpu.VMEM((rows, N * COLS), BF),
             pltpu.VMEM((2, N, RANK, COLS), BF),
-            pltpu.VMEM((2, N, RANK, COLS), BF),
-            pltpu.VMEM((2, N, RANK, COLS), BF),
-            pltpu.VMEM((4, N, RANK, 2 * RANK), F32),
+            pltpu.VMEM((2, 2, 4, 4, 32, COLS), BF),
+            pltpu.VMEM((2, 2, 2, 4, 16, COLS), BF),
+            pltpu.VMEM((2, 2, 2, 4, 32, COLS), BF),
+            pltpu.VMEM((2, 2, 4, 32, COLS), BF),
+            pltpu.VMEM((2, 2, 2, 16, COLS), BF),
+            pltpu.VMEM((2, 2, 2, 32, COLS), BF),
+            pltpu.VMEM((4, 4, 32, 128), F32),
+            pltpu.VMEM((4, 4, 32, 128), F32),
             pltpu.SemaphoreType.DMA,
-            pltpu.SemaphoreType.DMA((8, N)),
-            pltpu.SemaphoreType.DMA((8, N)),
+            pltpu.SemaphoreType.DMA((192,)),
+            pltpu.SemaphoreType.DMA((192,)),
         ],
         compiler_params=pltpu.CompilerParams(
-            collective_id=0, has_side_effects=True, vmem_limit_bytes=40 * 1024 * 1024
+            collective_id=0, has_side_effects=True, vmem_limit_bytes=60 * 1024 * 1024
         ),
         name="subspace",
     )(changes, start_t)
@@ -394,99 +549,118 @@
     )(pack, right_t)
 
 
-def merge_kernel(own, lall, rall, out, both, scaled, white, lsem, ssem, rsem):
+def merge_kernel(gram, lall, rall, order, out, chain, half, left, right, scaled, ssem, rsem):
     c = lax.axis_index("ckpt")
     side = lax.rem(c, 2)
+    even = side == 0
     other = c + 1 - 2 * side
+
+    def to_other(src, dst, sem):
+        return pltpu.make_async_remote_copy(
+            src_ref=src,
+            dst_ref=dst,
+            send_sem=ssem.at[sem],
+            recv_sem=rsem.at[sem],
+            device_id={"ckpt": other},
+            device_id_type=MESH,
+        )
+
     barrier = pltpu.get_barrier_semaphore()
     pl.semaphore_signal(barrier, inc=1, device_id={"ckpt": other}, device_id_type=MESH)
     pl.semaphore_wait(barrier, 1)
-    exchange = pltpu.make_async_remote_copy(
-        src_ref=own,
-        dst_ref=both.at[side],
-        send_sem=ssem,
-        recv_sem=rsem,
-        device_id={"ckpt": other},
-        device_id_type=MESH,
-    )
-    exchange.start()
-    keep = pltpu.make_async_copy(own, both.at[side], lsem)
-    keep.start()
-    keep.wait()
-    pltpu.make_async_remote_copy(
-        src_ref=own,
-        dst_ref=both.at[1 - side],
-        send_sem=ssem,
-        recv_sem=rsem,
-        device_id={"ckpt": other},
-        device_id_type=MESH,
-    ).wait_recv()
-    scaled[...] = lax.dot_general(
-        lall[:, :ROWS], both[0], (((0,), (0,)), ((), ())), preferred_element_type=F32
+
+    @pl.when(~even)
+    def _():
+        to_other(gram, chain.at[1, 0], 0).start()
+
+    def factors(step):
+        return (1.5 / 4.0, -0.5 / 64.0) if step == 0 else (1.5, -0.5)
+
+    def advance(dst, old, weights, lead, tail, tile):
+        @pl.loop(0, ALL // tile)
+        def _(i):
+            part = pl.ds(pl.multiple_of(i * tile, tile), tile)
+            product = jnp.dot(old[part, :], weights[...], preferred_element_type=F32)
+            dst[part, :] = (lead * old[part, :].astype(F32) + tail * product).astype(BF)
+
+    def apply(dst, old, grams, lead, tail, tile):
+        @pl.loop(0, ALL // tile)
+        def _(i):
+            part = pl.ds(pl.multiple_of(i * tile, tile), tile)
+            product = jnp.dot(grams[part, :], old[...], preferred_element_type=F32)
+            dst[part, :] = (lead * old[part, :].astype(F32) + tail * product).astype(BF)
+
+    for step in range(NS_ITERS - 1):
+        current = gram if step == 0 else chain.at[side, step]
+        advance(half, current, current, *factors(step), TILE)
+        advance(chain.at[side, step + 1], half, current, *factors(step), TILE)
+
+        @pl.when(~even)
+        def _():
+            to_other(chain.at[1, step + 1], chain.at[1, step + 1], step + 1).start()
+
+    @pl.when(even)
+    def _():
+        for step in range(NS_ITERS):
+            old = lall.at[:, :ROWS] if step == 0 else left.at[(step - 1) % 2]
+            current = gram if step == 0 else chain.at[0, step]
+            apply(left.at[step % 2], old, current, *factors(step), TILE)
+        for k in range(N):
+            block = pl.ds(k * RANK, RANK)
+            weight = (1 + order[k]).astype(F32) / N
+            middle_t = lall[block, ROWS : ROWS + RANK]
+            scaled[block, :] = (
+                weight * jnp.dot(middle_t, left[(NS_ITERS - 1) % 2, block, :], preferred_element_type=F32)
+            ).astype(BF)
+        to_other(scaled, scaled, 4).start()
+        for step in range(NS_ITERS):
+            to_other(chain.at[1, step], chain.at[1, step], step).wait_recv()
+            old = rall if step == 0 else right.at[(step - 1) % 2]
+            apply(right.at[step % 2], old, chain.at[1, step], *factors(step), TILE)
+        to_other(scaled, scaled, 4).wait_send()
+
+    @pl.when(~even)
+    def _():
+        for step in range(NS_ITERS):
+            old = rall if step == 0 else right.at[(step - 1) % 2]
+            current = gram if step == 0 else chain.at[1, step]
+            apply(right.at[step % 2], old, current, *factors(step), TILE)
+        for step in range(NS_ITERS):
+            to_other(chain.at[1, step], chain.at[1, step], step).wait_send()
+        to_other(scaled, scaled, 4).wait_recv()
+
+    out[...] = lax.dot_general(
+        scaled[...], right[(NS_ITERS - 1) % 2], (((0,), (0,)), ((), ())), preferred_element_type=F32
     ).astype(BF)
 
-    @pl.loop(0, 4)
-    def _(i):
-        part = pl.ds(pl.multiple_of(i * 256, 256), 256)
-        white[part, :] = jnp.dot(both[1, part, :], rall[...], preferred_element_type=F32).astype(BF)
-
-    out[...] = jnp.dot(scaled[...], white[...], preferred_element_type=F32).astype(BF)
-    exchange.wait_send()
-
-
-def merge(own, lall, rall):
+
+def merge(gram, lall, rall, edit_order):
     vmem = pl.BlockSpec(memory_space=pltpu.VMEM)
     return pl.pallas_call(
         merge_kernel,
         out_shape=jax.ShapeDtypeStruct((ROWS, COLS), BF),
-        in_specs=[vmem, vmem, vmem],
+        in_specs=[vmem, vmem, vmem, pl.BlockSpec(memory_space=pltpu.SMEM)],
         out_specs=vmem,
         scratch_shapes=[
-            pltpu.VMEM((2, ALL, ALL), BF),
-            pltpu.VMEM((ROWS, ALL), BF),
-            pltpu.VMEM((ALL, COLS), BF),
-            pltpu.SemaphoreType.DMA,
-            pltpu.SemaphoreType.DMA,
-            pltpu.SemaphoreType.DMA,
+            pltpu.VMEM((2, NS_ITERS, ALL, ALL), BF),
+            pltpu.VMEM((ALL, ALL), BF),
+            pltpu.VMEM((2, ALL, ROWS), BF),
+            pltpu.VMEM((2, ALL, COLS), BF),
+            pltpu.VMEM((ALL, ROWS), BF),
+            pltpu.SemaphoreType.DMA((5,)),
+            pltpu.SemaphoreType.DMA((5,)),
         ],
         compiler_params=pltpu.CompilerParams(
-            collective_id=2, has_side_effects=True, vmem_limit_bytes=40 * 1024 * 1024
+            collective_id=2, has_side_effects=True, vmem_limit_bytes=45 * 1024 * 1024
         ),
         name="merge",
-    )(own, lall, rall)
-
-
-def whitener(gram16):
-    def mul(a, b):
-        return jnp.dot(a.astype(BF), b.astype(BF), preferred_element_type=F32)
-
-    gram = gram16.astype(F32)
-    lead, tail = 1.5 / 4.0, -0.5 / 64.0
-    product = lead * jnp.eye(ALL, dtype=F32) + tail * gram
-    for step in range(NS_ITERS):
-        if step > 0:
-            lead, tail = 1.5, -0.5
-            product = lead * product + tail * mul(product, gram)
-        if step < NS_ITERS - 1:
-            half = lead * gram + tail * mul(gram, gram)
-            gram = lead * half + tail * mul(half, gram)
-    return product.astype(BF)
+    )(gram, lall, rall, edit_order)
 
 
 def body(deltas, start_basis, edit_order):
     pack, right_t = subspace(deltas[0], start_basis[0].T)
     lall, rall, gram = gather_stacks(pack, right_t)
-    white = whitener(gram)
-    weights = jnp.repeat((1 + edit_order).astype(F32) / N, RANK)
-    middle_t = lall[:, ROWS + RANK :].astype(F32) * weights[:, None]
-    block = jnp.arange(ALL) // RANK
-    same = block[:, None] == block[None, :]
-    even = lax.rem(lax.axis_index("ckpt"), 2) == 0
-    scale_t = jnp.where(
-        even, jnp.where(same, jnp.tile(middle_t, (1, N)), 0.0), jnp.eye(ALL, dtype=F32)
-    ).astype(BF)
-    own = dot_nt(white, scale_t).astype(BF)
-    return merge(own, lall, rall)
+    return merge(gram, lall, rall, edit_order)
 
 
 def solution(mesh):

time: 303 us -> 260 us (0.86)
  matrix products: 38.9 us -> 0 us
  local copies, waits for them, and re-layouts: 10.5 us -> 2.46 us
  Pallas kernels: 249 us -> 253 us
    dot_general x9 -> x0, matrix products: 38.9 us -> none  [the longest x8 34.2 us: mul(): return jnp.dot(a.astype(BF), b.astype(BF), preferred_element_type=F32)]
    pallas_call x1, Pallas kernels: 8.64 us -> 36.3 us  [merge(): pl.pallas_call(merge_kernel, out_shape=jax.ShapeDtypeStruct((ROWS, COLS),...]
    pallas_call x1, Pallas kernels: 143 us -> 120 us  [subspace(): pl.pallas_call(subspace_kernel, out_shape=(jax.ShapeDtypeStruct((RANK, PA...]
    another operation x2 -> x0, local copies, waits for them, and re-layouts: 5.49 us -> none  [body(): jnp.tile(middle_t, (1, N))]
where the time goes in v3:
time: 260 us; the launch traced here: 255 us
  Pallas kernels  253 us (97%)
    pallas_call x1, Pallas kernels, subspace(): pl.pallas_call(subspace_kernel, out_shape=(jax.ShapeDtypeStruct((RANK, PA...  120 us
    pallas_call x1, Pallas kernels, gather_stacks(): pl.pallas_call(gather_kernel, out_shape=(jax.ShapeDtypeStruct((ALL, PACK)...  96.6 us
    pallas_call x1, Pallas kernels, merge(): pl.pallas_call(merge_kernel, out_shape=jax.ShapeDtypeStruct((ROWS, COLS),...  36.3 us

profile of v3, /device:TPU:8, one launch (start us, length us, event | category | flops | bytes accessed | tf_op | source)
XLA Modules:
  0.0 255.3 jit_solution(134860726435715545)
XLA Ops:
  0.0 0.0 copy-start.2
  0.0 119.9 %subspace.1 = (bf16[64,384]{1,0:T(8,128)(2,1)}, bf16[64,896]{1,0:T(8,128)(2,1)}) custom-call(bf16[256,14336]{1,0:T(8,128)(2,1)} %bitcast.4, bf16[64,896]{1,0:T(8,128)(2,1)} %bitcast.5), custom_call_target="tpu_custom_call" | custom-call | tf_op jit(solution)/shard_map/subspace/pallas_call | solution.py:322
  119.9 0.0 copy-start
  119.9 0.9 copy-done
  120.8 0.0 copy-start.1
  120.8 0.8 copy-done.1
  121.6 96.6 %gather_stacks.1 = (bf16[1024,384]{1,0:T(8,128)(2,1)S(1)}, bf16[1024,896]{1,0:T(8,128)(2,1)S(1)}, bf16[1024,1024]{1,0:T(8,128)(2,1)S(1)}) custom-call(bf16[64,384]{1,0:T(8,128)(2,1)S(1)} %copy-done.1, bf16[64,896]{1,0:T(8,128)(2,1)S(1)} %copy-done), custom_call_target="tpu_custom_call" | custom-call | tf_op jit(solution)/shard_map/gather_stacks/pallas_call | solution.py:526
  218.2 0.0 copy-done.2
  218.2 36.3 %merge.1 = bf16[256,896]{1,0:T(8,128)(2,1)S(1)} custom-call(bf16[1024,1024]{1,0:T(8,128)(2,1)S(1)} %get-tuple-element.12.gram, bf16[1024,384]{1,0:T(8,128)(2,1)S(1)} %get-tuple-element.13.lall, bf16[1024,896]{1,0:T(8,128)(2,1)S(1)} %get-tuple-element.14.rall, s32[16]{0:T(128)S(1)} %copy-done.2), custom_call_target="tpu_custom_call" | custom-call | tf_op jit(solution)/shard_map/merge/pallas_call | solution.py:639
  254.6 0.8 copy.5
Async XLA Ops:
  0.0 218.2 %copy-start.2 = (s32[16]{0:T(128)S(1)}, s32[16]{0:T(128)}, u32[]{:S(2)}) copy-start(s32[16]{0:T(128)} %order.1) | copy-start | bytes 196
  119.9 0.9 copy-start
  120.8 0.8 copy-start.1

commit v4 on v3

v4 whole, which is shorter than its diff:
```python
import functools

import jax
import jax.numpy as jnp
from jax import lax
from jax.experimental import pallas as pl
from jax.experimental.pallas import tpu as pltpu
from jax.sharding import PartitionSpec as P

RANK = 64
NS_ITERS = 4
N = 16
COLS = 896
ROWS = 256
PACK = ROWS + 2 * RANK
ALL = N * RANK
TILE = 256
BF = jnp.bfloat16
F32 = jnp.float32
MESH = pl.DeviceIdType.MESH
HIGHEST = lax.Precision.HIGHEST
NT = (((1,), (1,)), ((), ()))


def dot_nt(a, b, precision=None):
    return lax.dot_general(a, b, NT, precision=precision, preferred_element_type=F32)


def factor_start(gram_wide):
    row = lax.broadcasted_iota(jnp.int32, (RANK, 2 * RANK), 0)
    lane = lax.broadcasted_iota(jnp.int32, (RANK, 2 * RANK), 1)
    return gram_wide + jnp.where(row == lane, 1.0, 0.0)


def factor_steps(work, first, last):
    row = lax.broadcasted_iota(jnp.int32, (RANK, 2 * RANK), 0)
    lane = lax.broadcasted_iota(jnp.int32, (RANK, 2 * RANK), 1)

    def step(j, w):
        pivot_row = jnp.sum(jnp.where(row == j, w, 0.0), axis=0, keepdims=True)
        column = jnp.sum(jnp.where(lane == j + RANK, w, 0.0), axis=1, keepdims=True)
        pivot = jnp.sum(jnp.where(lane[:1] == j + RANK, pivot_row, 0.0), axis=1, keepdims=True)
        ratio = jnp.where(row[:, :1] > j, column, 0.0) / pivot
        return w - ratio * pivot_row

    return lax.fori_loop(first, last, step, work)


def factor_end(work):
    row = lax.broadcasted_iota(jnp.int32, (RANK, 2 * RANK), 0)
    lane = lax.broadcasted_iota(jnp.int32, (RANK, 2 * RANK), 1)
    diagonal = jnp.sum(jnp.where(lane == row + RANK, work, 0.0), axis=1, keepdims=True)
    return work * lax.rsqrt(diagonal)


def xor(a, b):
    return sum(bit * lax.rem(lax.div(a, bit) + lax.div(b, bit), 2) for bit in (1, 2, 4, 8))


OFFSETS = (0, -1, 1, 2)
FAR_FIRST = (2, 1, -1, 0)


class Plane:
    def __init__(self, ssem, rsem):
        self.ssem, self.rsem = ssem, rsem
        self.r = lax.axis_index("rows")
        self.x, self.y = lax.rem(self.r, 4), lax.div(self.r, 4)
        self.sends = []
        self.tasks = []

    def place(self, axis, da, db):
        dx, dy = (da, db) if axis == 0 else (db, da)
        return lax.rem(self.y + dy + 4, 4) * 4 + lax.rem(self.x + dx + 4, 4)

    def spot(self, axis, delta):
        return lax.rem((self.x if axis == 0 else self.y) + delta + 4, 4)

    def copy(self, src, dst, sem, to):
        return pltpu.make_async_remote_copy(
            src_ref=src,
            dst_ref=dst,
            send_sem=self.ssem.at[sem],
            recv_sem=self.rsem.at[sem],
            device_id={"rows": to},
            device_id_type=MESH,
        )

    def go(self, src, dst, sem, to):
        copy = self.copy(src, dst, sem, to)
        copy.start()
        self.sends.append(copy)

    def got(self, dst, sem):
        self.copy(dst, dst, sem, self.r).wait_recv()

    def tick(self):
        if self.tasks:
            self.tasks.pop(0)()

    def flush(self):
        while self.tasks:
            self.tick()

    def finish(self):
        for copy in self.sends:
            copy.wait_send()

    def gather(self, half, quarter, base, ready):
        def send(ref, h, slot, da, db):
            self.go(ref, ref, base + 20 * h + slot, self.place(h, da, db))

        def take(ref, h, slot):
            self.got(ref, base + 20 * h + slot)

        def spread(h, j):
            origin = self.place(h, OFFSETS[j], 0)
            send(half(h, origin), h, 4 + j, 0, 1)
            send(half(h, origin), h, 8 + j, 0, -1)

        def relay(h, j):
            origin = self.place(h, OFFSETS[j], -1)
            take(half(h, origin), h, 4 + j)
            send(quarter(h, origin, 0), h, 12 + j, 0, 1)
            origin = self.place(h, OFFSETS[j], 1)
            take(half(h, origin), h, 8 + j)
            send(quarter(h, origin, 1), h, 16 + j, 0, -1)

        for h in range(2):
            send(half(h, self.r), h, 0, 1, 0)
            send(half(h, self.r), h, 1, -1, 0)
            spread(h, 0)
        ready([(0, 0)])
        self.tick()
        for h in range(2):
            origin = self.place(h, -1, 0)
            take(half(h, origin), h, 0)
            send(quarter(h, origin, 0), h, 2, 1, 0)
            origin = self.place(h, 1, 0)
            take(half(h, origin), h, 1)
            send(quarter(h, origin, 1), h, 3, -1, 0)
        for h in range(2):
            spread(h, 1)
            spread(h, 2)
        self.tick()
        for h in range(2):
            relay(h, 0)
        for h in range(2):
            origin = self.place(h, 2, 0)
            take(quarter(h, origin, 0), h, 2)
            take(quarter(h, origin, 1), h, 3)
            spread(h, 3)
        ready([(-1, 0), (1, 0), (0, -1), (0, 1)])
        self.tick()
        for j in (1, 2):
            for h in range(2):
                relay(h, j)
        self.tick()
        ready([(-1, -1), (1, -1), (-1, 1), (1, 1)])
        for h in range(2):
            relay(h, 3)
        self.tick()
        groups = ([(0, 2), (2, 0)], [(-1, 2), (2, -1)], [(1, 2), (2, 1)], [(2, 2)])
        for j in range(4):
            for h in range(2):
                origin = self.place(h, OFFSETS[j], 2)
                take(quarter(h, origin, 0), h, 12 + j)
                take(quarter(h, origin, 1), h, 16 + j)
            ready(groups[j])
        self.flush()

    def scatter(self, part, y, t1, t2, s1, u1, u2, base):
        done = set()

        def make(dx, dy):
            if (dx, dy) in done:
                return
            done.add((dx, dy))
            xs, ys = self.spot(0, dx), self.spot(1, dy)
            value = part(ys * 4 + xs).astype(BF)
            y[0, ys, xs] = value[:32]
            y[1, xs, ys] = value[32:]

        def low(q):
            return pl.ds(16 * q, 16)

        for i, j in enumerate(FAR_FIRST):
            for h in range(2):
                make(*((j, 2) if h == 0 else (2, j)))
                b, a = self.spot(1 - h, 2), self.spot(h, j)
                for q in range(2):
                    self.go(
                        y.at[h, b, a, low(q)], t1.at[h, q, i], base + 20 * h + 4 * q + i,
                        self.place(h, 0, 1 - 2 * q),
                    )
        self.tick()
        for i, j in enumerate(FAR_FIRST):
            for h in range(2):
                for q in range(2):
                    delta = 1 - 2 * q
                    make(*((j, delta) if h == 0 else (delta, j)))
                    b, a = self.spot(1 - h, delta), self.spot(h, j)
                    self.got(t1.at[h, q, i], base + 20 * h + 4 * q + i)
                    y[h, b, a, low(q)] = (
                        y[h, b, a, low(q)].astype(F32) + t1[h, q, i].astype(F32)
                    ).astype(BF)
                    self.go(
                        y.at[h, b, a], t2.at[h, q, i], base + 20 * h + 8 + 4 * q + i,
                        self.place(h, 0, delta),
                    )
            self.tick()
        make(0, 0)
        self.flush()
        result = [None, None]
        for i, j in enumerate(FAR_FIRST):
            for h in range(2):
                b, a = self.spot(1 - h, 0), self.spot(h, j)
                make(*((j, 0) if h == 0 else (0, j)))
                self.got(t2.at[h, 0, i], base + 20 * h + 8 + i)
                self.got(t2.at[h, 1, i], base + 20 * h + 12 + i)
                total = y[h, b, a].astype(F32) + t2[h, 0, i].astype(F32) + t2[h, 1, i].astype(F32)
                if j == 2:
                    s1[h, i] = total.astype(BF)
                    for q in range(2):
                        self.go(
                            s1.at[h, i, low(q)], u1.at[h, q], base + 20 * h + 16 + q,
                            self.place(h, 1 - 2 * q, 0),
                        )
                elif j != 0:
                    q = 0 if j == 1 else 1
                    self.got(u1.at[h, q], base + 20 * h + 16 + q)
                    s1[h, i] = total.astype(BF)
                    s1[h, i, low(q)] = (
                        total[16 * q : 16 * q + 16] + u1[h, q].astype(F32)
                    ).astype(BF)
                    self.go(
                        s1.at[h, i], u2.at[h, q], base + 20 * h + 18 + q, self.place(h, j, 0)
                    )
                else:
                    result[h] = total
        for h in range(2):
            for q in range(2):
                self.got(u2.at[h, q], base + 20 * h + 18 + q)
                result[h] = result[h] + u2[h, q].astype(F32)
        return jnp.concatenate(result, axis=0)


def merge_kernel(
    d_hbm, b_ref, order, out,
    d, ag, y, t1, t2, s1, u1, u2, gx, gy,
    lall, fall, swp, raw, rall, gram, glp, grp, grs, blk, zst,
    chain, half, left, right, scaled,
    dsem, ssem, rsem, cs, cr, ssem2, rsem2,
):
    plane = Plane(ssem, rsem)
    me = r = plane.r
    c = lax.axis_index("ckpt")
    side = lax.rem(c, 2)
    even = side == 0
    other = c + 1 - 2 * side
    load = pltpu.make_async_copy(d_hbm, d, dsem.at[0])
    load.start()
    barrier = pltpu.get_barrier_semaphore()

    @pl.loop(1, N)
    def _(k):
        pl.semaphore_signal(barrier, inc=1, device_id={"rows": lax.rem(r + k, N)}, device_id_type=MESH)
        pl.semaphore_signal(barrier, inc=1, device_id={"ckpt": lax.rem(c + k, N)}, device_id_type=MESH)

    ag[0, me] = b_ref[...]
    pl.semaphore_wait(barrier, 2 * N - 2)

    def columns(j):
        return pl.ds(pl.multiple_of(j * COLS, 128), COLS)

    def left_product(sweep, base):
        total = [jnp.zeros((RANK, ROWS), F32)]

        def ready(sources):
            for dx, dy in sources:
                source = plane.place(0, dx, dy)
                if (dx, dy) == (0, 0) and sweep == 0:
                    load.wait()
                total[0] = total[0] + dot_nt(ag[sweep, source], d[:, columns(source)])

        plane.gather(
            lambda h, o: ag.at[sweep, o, pl.ds(32 * h, 32)],
            lambda h, o, q: ag.at[sweep, o, pl.ds(32 * h + 16 * q, 16)],
            base,
            ready,
        )
        return total[0]

    def right_product(left16, sweep, base, label):
        return plane.scatter(
            lambda j: jnp.dot(left16, d[:, columns(label(j))], preferred_element_type=F32),
            *(ref.at[sweep] for ref in (y, t1, t2, s1, u1, u2)),
            base,
        )

    def exchange(buffer, axis, base):
        mine = plane.spot(axis, 0)
        for k in range(1, 4):
            plane.go(buffer.at[mine], buffer.at[mine], base + k, plane.place(axis, k, 0))

    def collect(buffer, axis, base):
        for k in range(1, 4):
            plane.got(buffer.at[plane.spot(axis, -k)], base + k)
        return (buffer[0] + buffer[1]) + (buffer[2] + buffer[3])

    facts = {}

    def gram_start(value, index):
        wide = dot_nt(value, jnp.concatenate([jnp.zeros_like(value), value], axis=0), HIGHEST)
        gx[index, plane.x] = pltpu.roll(wide[:32], RANK, 1) + wide[32:]
        exchange(gx.at[index], 0, 160 + 8 * index)

        def middle():
            gy[index, plane.y] = collect(gx.at[index], 0, 160 + 8 * index)
            exchange(gy.at[index], 1, 164 + 8 * index)

        def begin():
            total = collect(gy.at[index], 1, 164 + 8 * index)
            on_right = lax.broadcasted_iota(jnp.int32, (32, 128), 1) >= RANK
            upper = jnp.where(on_right, pltpu.roll(total, RANK, 1), 0.0)
            lower = jnp.where(on_right, total, 0.0)
            work = factor_start(jnp.concatenate([upper, lower], axis=0))
            facts[index] = factor_steps(work, 0, 16)

        def go_on(first):
            facts[index] = factor_steps(facts[index], first, first + 16)
            if first == 48:
                facts[index] = factor_end(facts[index])

        plane.tasks = [middle, begin] + [functools.partial(go_on, first) for first in (16, 32, 48)]

    def apply_inverse(index, value):
        return jnp.dot(facts[index][:, :RANK], value, precision=HIGHEST)

    left_raw = left_product(0, 0)
    gram_start(left_raw, 0)
    right_sum = right_product(left_raw.astype(BF), 0, 80, lambda j: j)
    right_raw = apply_inverse(0, right_sum)
    ag[1, me] = right_raw.astype(BF)
    gram_start(right_raw, 1)
    left_raw = apply_inverse(1, left_product(1, 40))
    gram_start(left_raw, 2)
    right_raw = apply_inverse(2, right_product(left_raw.astype(BF), 1, 120, lambda j: xor(j, c)))

    def rows64(i):
        return pl.ds(pl.multiple_of(i * RANK, RANK), RANK)

    def rows32(i):
        return pl.ds(pl.multiple_of(i * 32, 32), 32)

    def tile_of(i):
        return lax.rem(i, 2) * 512, pl.ds(pl.multiple_of(lax.div(i, 2) * 128, 128), 128)

    def send(axis, mine, src, dst, phase, k):
        return pltpu.make_async_remote_copy(
            src_ref=src,
            dst_ref=dst,
            send_sem=cs.at[phase, k],
            recv_sem=cr.at[phase, mine],
            device_id={axis: lax.rem(mine + k, N)},
            device_id_type=MESH,
        )

    def arrival(axis, buffer, phase, source):
        pltpu.make_async_remote_copy(
            src_ref=buffer,
            dst_ref=buffer,
            send_sem=cs.at[phase, 0],
            recv_sem=cr.at[phase, source],
            device_id={axis: source},
            device_id_type=MESH,
        ).wait_recv()

    def swap():
        return pltpu.make_async_remote_copy(
            src_ref=swp,
            dst_ref=raw.at[r],
            send_sem=cs.at[5, 0],
            recv_sem=cr.at[5, 0],
            device_id={"ckpt": xor(r, c)},
            device_id_type=MESH,
        )

    right16 = right_raw.astype(BF)

    @pl.when(r == 0)
    def _():
        raw[0] = right16

    @pl.when(r != 0)
    def _():
        swp[...] = right16
        pltpu.make_async_remote_copy(
            src_ref=swp,
            dst_ref=raw.at[r],
            send_sem=cs.at[5, 0],
            recv_sem=cr.at[5, 0],
            device_id={"ckpt": xor(r, c)},
            device_id_type=MESH,
        ).start()

    gram_start(right_raw, 3)
    lall[rows64(c)] = apply_inverse(2, left_raw).astype(BF)

    @pl.loop(1, N)
    def _(k):
        send("ckpt", c, lall.at[rows64(c)], lall.at[rows64(c)], 0, k).start()

    plane.tick()

    def finish_fact():
        fall[rows64(c)] = facts[3].astype(BF)

        @pl.loop(1, N)
        def _(k):
            send("ckpt", c, fall.at[rows64(c)], fall.at[rows64(c)], 1, k).start()

    def left_gram():
        @pl.loop(1, N)
        def _(k):
            source = lax.rem(c + N - k, N)
            arrival("ckpt", lall.at[rows64(source)], 0, source)

        for part in range(2):
            strip = lall[pl.ds(pl.multiple_of(part * 512 + c * 32, 32), 32), :]
            product = dot_nt(strip, lall[...]).astype(BF)
            for q in range(8):
                glp[2 * q + part] = product[:, q * 128 : (q + 1) * 128]

        @pl.loop(1, N)
        def _(k):
            send("rows", r, glp.at[lax.rem(r + k, N)], grs.at[0, r], 2, k).start()

    plane.tasks = plane.tasks + [finish_fact, left_gram]

    @pl.when(r != 0)
    def _():
        swap().wait_recv()

    plane.gather(
        lambda h, o: raw.at[o, pl.ds(32 * h, 32)],
        lambda h, o, q: raw.at[o, pl.ds(32 * h + 16 * q, 16)],
        192,
        lambda sources: None,
    )

    @pl.loop(1, N)
    def _(k):
        source = lax.rem(c + N - k, N)
        arrival("ckpt", fall.at[rows64(source)], 1, source)

    @pl.loop(0, N)
    def _(o):
        e = xor(o, c)
        rall[rows64(e), :] = jnp.dot(
            fall[rows64(e), :RANK], raw[o], preferred_element_type=F32
        ).astype(BF)

    first_row, pair = tile_of(r)
    pair_rows = pl.ds(pl.multiple_of(lax.div(r, 2) * 128, 128), 128)
    half_rows = pl.ds(pl.multiple_of(first_row, 512), 512)
    grp[...] = dot_nt(rall[half_rows, :], rall[pair_rows, :]).astype(BF)

    @pl.loop(1, N)
    def _(k):
        send("ckpt", c, grp.at[rows32(lax.rem(c + k, N))], grs.at[1, c], 3, k).start()

    def total_of(axis, mine, which, phase, first):
        def step(k, value):
            source = lax.rem(mine + N - k, N)
            arrival(axis, grs.at[which, source], phase, source)
            return value + grs[which, source].astype(F32)

        return lax.fori_loop(1, N, step, first.astype(F32)).astype(BF)

    blk[0] = total_of("rows", r, 0, 2, glp[r])
    blk[1] = total_of("ckpt", c, 1, 3, grp[rows32(c)])

    @pl.loop(1, N)
    def _(k):
        send("ckpt", c, blk.at[lax.rem(c + k, 2)], zst.at[rows32(c)], 4, k).start()

    zst[rows32(c)] = blk[side]

    @pl.loop(1, N)
    def _(k):
        source = lax.rem(c + N - k, N)
        arrival("ckpt", zst.at[rows32(source)], 4, source)

    gram[half_rows, pair] = zst[...]

    def gram_part(o, start, size):
        row, lanes = tile_of(o)
        return gram.at[pl.ds(pl.multiple_of(row + start, 128), size), lanes]

    plane.gather(
        lambda h, o: gram_part(o, 256 * h, 256),
        lambda h, o, q: gram_part(o, 256 * h + 128 * q, 128),
        232,
        lambda sources: None,
    )

    def to_other(src, dst, sem):
        return pltpu.make_async_remote_copy(
            src_ref=src,
            dst_ref=dst,
            send_sem=ssem2.at[sem],
            recv_sem=rsem2.at[sem],
            device_id={"ckpt": other},
            device_id_type=MESH,
        )

    @pl.when(~even)
    def _():
        to_other(gram, chain.at[1, 0], 0).start()

    def factors(step):
        return (1.5 / 4.0, -0.5 / 64.0) if step == 0 else (1.5, -0.5)

    def advance(dst, old, weights, lead, tail, tile):
        @pl.loop(0, ALL // tile)
        def _(i):
            part = pl.ds(pl.multiple_of(i * tile, tile), tile)
            product = jnp.dot(old[part, :], weights[...], preferred_element_type=F32)
            dst[part, :] = (lead * old[part, :].astype(F32) + tail * product).astype(BF)

    def apply(dst, old, grams, lead, tail, tile):
        @pl.loop(0, ALL // tile)
        def _(i):
            part = pl.ds(pl.multiple_of(i * tile, tile), tile)
            product = jnp.dot(grams[part, :], old[...], preferred_element_type=F32)
            dst[part, :] = (lead * old[part, :].astype(F32) + tail * product).astype(BF)

    for step in range(NS_ITERS - 1):
        current = gram if step == 0 else chain.at[side, step]
        advance(half, current, current, *factors(step), TILE)
        advance(chain.at[side, step + 1], half, current, *factors(step), TILE)

        @pl.when(~even)
        def _():
            to_other(chain.at[1, step + 1], chain.at[1, step + 1], step + 1).start()

    @pl.when(even)
    def _():
        for step in range(NS_ITERS):
            old = lall if step == 0 else left.at[(step - 1) % 2]
            current = gram if step == 0 else chain.at[0, step]
            apply(left.at[step % 2], old, current, *factors(step), TILE)
        for k in range(N):
            block = pl.ds(k * RANK, RANK)
            weight = (1 + order[k]).astype(F32) / N
            white = left[(NS_ITERS - 1) % 2, block, :]
            white = jnp.concatenate([jnp.zeros_like(white), white], axis=0)
            scaled[block, :] = (
                weight * jnp.dot(fall[block, :], white, preferred_element_type=F32)
            ).astype(BF)
        to_other(scaled, scaled, 4).start()
        for step in range(NS_ITERS):
            to_other(chain.at[1, step], chain.at[1, step], step).wait_recv()
            old = rall if step == 0 else right.at[(step - 1) % 2]
            apply(right.at[step % 2], old, chain.at[1, step], *factors(step), TILE)
        to_other(scaled, scaled, 4).wait_send()

    @pl.when(~even)
    def _():
        for step in range(NS_ITERS):
            old = rall if step == 0 else right.at[(step - 1) % 2]
            current = gram if step == 0 else chain.at[1, step]
            apply(right.at[step % 2], old, current, *factors(step), TILE)
        for step in range(NS_ITERS):
            to_other(chain.at[1, step], chain.at[1, step], step).wait_send()
        to_other(scaled, scaled, 4).wait_recv()

    out[...] = lax.dot_general(
        scaled[...], right[(NS_ITERS - 1) % 2], (((0,), (0,)), ((), ())), preferred_element_type=F32
    ).astype(BF)

    @pl.when(r != 0)
    def _():
        swap().wait_send()

    @pl.loop(1, N)
    def _(k):
        send("ckpt", c, lall.at[rows64(c)], lall.at[rows64(c)], 0, k).wait_send()
        send("ckpt", c, fall.at[rows64(c)], fall.at[rows64(c)], 1, k).wait_send()
        send("rows", r, glp.at[0], grs.at[0, r], 2, k).wait_send()
        send("ckpt", c, grp.at[rows32(c)], grs.at[1, c], 3, k).wait_send()
        send("ckpt", c, blk.at[0], zst.at[rows32(c)], 4, k).wait_send()

    plane.finish()


def body(deltas, start_basis, edit_order):
    vmem = pl.BlockSpec(memory_space=pltpu.VMEM)
    return pl.pallas_call(
        merge_kernel,
        out_shape=jax.ShapeDtypeStruct((ROWS, COLS), BF),
        in_specs=[
            pl.BlockSpec(memory_space=pl.ANY), vmem, pl.BlockSpec(memory_space=pltpu.SMEM),
        ],
        out_specs=vmem,
        scratch_shapes=[
            pltpu.VMEM((ROWS, N * COLS), BF),
            pltpu.VMEM((2, N, RANK, COLS), BF),
            pltpu.VMEM((2, 2, 4, 4, 32, COLS), BF),
            pltpu.VMEM((2, 2, 2, 4, 16, COLS), BF),
            pltpu.VMEM((2, 2, 2, 4, 32, COLS), BF),
            pltpu.VMEM((2, 2, 4, 32, COLS), BF),
            pltpu.VMEM((2, 2, 2, 16, COLS), BF),
            pltpu.VMEM((2, 2, 2, 32, COLS), BF),
            pltpu.VMEM((4, 4, 32, 128), F32),
            pltpu.VMEM((4, 4, 32, 128), F32),
            pltpu.VMEM((ALL, ROWS), BF),
            pltpu.VMEM((ALL, 2 * RANK), BF),
            pltpu.VMEM((RANK, COLS), BF),
            pltpu.VMEM((N, RANK, COLS), BF),
            pltpu.VMEM((ALL, COLS), BF),
            pltpu.VMEM((ALL, ALL), BF),
            pltpu.VMEM((N, 32, 128), BF),
            pltpu.VMEM((512, 128), BF),
            pltpu.VMEM((2, N, 32, 128), BF),
            pltpu.VMEM((2, 32, 128), BF),
            pltpu.VMEM((512, 128), BF),
            pltpu.VMEM((2, NS_ITERS, ALL, ALL), BF),
            pltpu.VMEM((ALL, ALL), BF),
            pltpu.VMEM((2, ALL, ROWS), BF),
            pltpu.VMEM((2, ALL, COLS), BF),
            pltpu.VMEM((ALL, ROWS), BF),
            pltpu.SemaphoreType.DMA((1,)),
            pltpu.SemaphoreType.DMA((272,)),
            pltpu.SemaphoreType.DMA((272,)),
            pltpu.SemaphoreType.DMA((6, N)),
            pltpu.SemaphoreType.DMA((6, N)),
            pltpu.SemaphoreType.DMA((5,)),
            pltpu.SemaphoreType.DMA((5,)),
        ],
        compiler_params=pltpu.CompilerParams(
            collective_id=0, has_side_effects=True, vmem_limit_bytes=62 * 1024 * 1024
        ),
        name="merge",
    )(deltas[0], start_basis[0].T, edit_order)


def solution(mesh):
    return jax.shard_map(
        body,
        mesh=mesh,
        in_specs=(P("ckpt", "rows", None), P("ckpt", "rows", None), P()),
        out_specs=P("rows", "ckpt"),
        check_vma=False,
    )
```

time: 260 us -> 202 us (0.78); the launches traced: 255 us -> 202 us
  Pallas kernels: 253 us -> 200 us
    pallas_call x3 -> x1, Pallas kernels: 253 us -> 200 us  [body(): pl.pallas_call(merge_kernel, out_shape=jax.ShapeDtypeStruct((ROWS, COLS),...]
where the time goes in v4:
time: 202 us
  Pallas kernels  200 us (99%)
    pallas_call x1, Pallas kernels, body(): pl.pallas_call(merge_kernel, out_shape=jax.ShapeDtypeStruct((ROWS, COLS),...  200 us

profile of v4, /device:TPU:8, one launch (start us, length us, event | category | flops | bytes accessed | tf_op | source)
XLA Modules:
  0.0 201.8 jit_solution(13751370820294254613)
XLA Ops:
  0.0 200.0 %merge.1 = bf16[256,896]{1,0:T(8,128)(2,1)} custom-call(bf16[256,14336]{1,0:T(8,128)(2,1)} %bitcast.4, bf16[64,896]{1,0:T(8,128)(2,1)} %bitcast.5, s32[16]{0:T(128)} %order.1), custom_call_target="tpu_custom_call" | custom-call | tf_op jit(solution)/shard_map/merge/pallas_call | solution.py:600
  200.0 1.8 copy.5

commit v5 on v4

--- a/solution.py
+++ b/solution.py
@@ -14,7 +14,8 @@
 ROWS = 256
 PACK = ROWS + 2 * RANK
 ALL = N * RANK
-TILE = 256
+TILE = 512
+PIVOTS = 4
 BF = jnp.bfloat16
 F32 = jnp.float32
 MESH = pl.DeviceIdType.MESH
@@ -36,14 +37,34 @@
     row = lax.broadcasted_iota(jnp.int32, (RANK, 2 * RANK), 0)
     lane = lax.broadcasted_iota(jnp.int32, (RANK, 2 * RANK), 1)
 
-    def step(j, w):
-        pivot_row = jnp.sum(jnp.where(row == j, w, 0.0), axis=0, keepdims=True)
-        column = jnp.sum(jnp.where(lane == j + RANK, w, 0.0), axis=1, keepdims=True)
-        pivot = jnp.sum(jnp.where(lane[:1] == j + RANK, pivot_row, 0.0), axis=1, keepdims=True)
-        ratio = jnp.where(row[:, :1] > j, column, 0.0) / pivot
-        return w - ratio * pivot_row
-
-    return lax.fori_loop(first, last, step, work)
+    def step(i, w):
+        p = [PIVOTS * i + k for k in range(PIVOTS)]
+        rows = [jnp.sum(jnp.where(row == p[k], w, 0.0), axis=0, keepdims=True) for k in range(PIVOTS)]
+        cols = [
+            jnp.sum(jnp.where(lane == p[k] + RANK, w, 0.0), axis=1, keepdims=True)
+            for k in range(PIVOTS)
+        ]
+        block = {
+            (k, m): jnp.sum(jnp.where(lane[:1] == p[m] + RANK, rows[k], 0.0), axis=1, keepdims=True)
+            for k in range(PIVOTS)
+            for m in range(k, PIVOTS)
+        }
+        inverse = []
+        for k in range(PIVOTS):
+            inverse.append(1.0 / block[k, k])
+            for n in range(k + 1, PIVOTS):
+                ratio = block[k, n] * inverse[k]
+                rows[n] = rows[n] - ratio * rows[k]
+                for m in range(n, PIVOTS):
+                    block[n, m] = block[n, m] - ratio * block[k, m]
+        for k in range(PIVOTS):
+            ratio = jnp.where(row[:, :1] > p[k], cols[k], 0.0) * inverse[k]
+            for m in range(k + 1, PIVOTS):
+                cols[m] = cols[m] - ratio * block[k, m]
+            w = w - ratio * rows[k]
+        return w
+
+    return lax.fori_loop(first // PIVOTS, last // PIVOTS, step, work)
 
 
 def factor_end(work):
@@ -106,7 +127,7 @@
         for copy in self.sends:
             copy.wait_send()
 
-    def gather(self, half, quarter, base, ready):
+    def gather(self, half, quarter, base, ready, landed=None):
         def send(ref, h, slot, da, db):
             self.go(ref, ref, base + 20 * h + slot, self.place(h, da, db))
 
@@ -127,6 +148,8 @@
             send(quarter(h, origin, 1), h, 16 + j, 0, -1)
 
         for h in range(2):
+            if landed is not None:
+                landed(h)
             send(half(h, self.r), h, 0, 1, 0)
             send(half(h, self.r), h, 1, -1, 0)
             spread(h, 0)
@@ -376,12 +399,12 @@
             device_id_type=MESH,
         ).wait_recv()
 
-    def swap():
+    def swap(h):
         return pltpu.make_async_remote_copy(
-            src_ref=swp,
-            dst_ref=raw.at[r],
-            send_sem=cs.at[5, 0],
-            recv_sem=cr.at[5, 0],
+            src_ref=swp.at[pl.ds(32 * h, 32)],
+            dst_ref=raw.at[r, pl.ds(32 * h, 32)],
+            send_sem=cs.at[5, h],
+            recv_sem=cr.at[5, h],
             device_id={"ckpt": xor(r, c)},
             device_id_type=MESH,
         )
@@ -395,14 +418,8 @@
     @pl.when(r != 0)
     def _():
         swp[...] = right16
-        pltpu.make_async_remote_copy(
-            src_ref=swp,
-            dst_ref=raw.at[r],
-            send_sem=cs.at[5, 0],
-            recv_sem=cr.at[5, 0],
-            device_id={"ckpt": xor(r, c)},
-            device_id_type=MESH,
-        ).start()
+        swap(0).start()
+        swap(1).start()
 
     gram_start(right_raw, 3)
     lall[rows64(c)] = apply_inverse(2, left_raw).astype(BF)
@@ -438,15 +455,17 @@
 
     plane.tasks = plane.tasks + [finish_fact, left_gram]
 
-    @pl.when(r != 0)
-    def _():
-        swap().wait_recv()
+    def landed(h):
+        @pl.when(r != 0)
+        def _():
+            swap(h).wait_recv()
 
     plane.gather(
         lambda h, o: raw.at[o, pl.ds(32 * h, 32)],
         lambda h, o, q: raw.at[o, pl.ds(32 * h + 16 * q, 16)],
         192,
         lambda sources: None,
+        landed,
     )
 
     @pl.loop(1, N)
@@ -582,7 +601,8 @@
 
     @pl.when(r != 0)
     def _():
-        swap().wait_send()
+        swap(0).wait_send()
+        swap(1).wait_send()
 
     @pl.loop(1, N)
     def _(k):
@@ -640,7 +660,7 @@
             pltpu.SemaphoreType.DMA((5,)),
         ],
         compiler_params=pltpu.CompilerParams(
-            collective_id=0, has_side_effects=True, vmem_limit_bytes=62 * 1024 * 1024
+            collective_id=0, has_side_effects=True, vmem_limit_bytes=55 * 1024 * 1024
         ),
         name="merge",
     )(deltas[0], start_basis[0].T, edit_order)

time: 202 us -> 186 us (0.921)
  Pallas kernels: 200 us -> 184 us
    pallas_call x1, Pallas kernels: 200 us -> 184 us  [body(): pl.pallas_call(merge_kernel, out_shape=jax.ShapeDtypeStruct((ROWS, COLS),...]
where the time goes in v5:
time: 186 us
  Pallas kernels  184 us (99%)
    pallas_call x1, Pallas kernels, body(): pl.pallas_call(merge_kernel, out_shape=jax.ShapeDtypeStruct((ROWS, COLS),...  184 us

profile of v5, /device:TPU:8, one launch (start us, length us, event | category | flops | bytes accessed | tf_op | source)
XLA Modules:
  0.0 186.2 jit_solution(13001023635328924350)
XLA Ops:
  0.0 184.4 %merge.1 = bf16[256,896]{1,0:T(8,128)(2,1)} custom-call(bf16[256,14336]{1,0:T(8,128)(2,1)} %bitcast.4, bf16[64,896]{1,0:T(8,128)(2,1)} %bitcast.5, s32[16]{0:T(128)} %order.1), custom_call_target="tpu_custom_call" | custom-call | tf_op jit(solution)/shard_map/merge/pallas_call | solution.py:620
  184.4 1.8 copy.5

commit v6 on v5

--- a/solution.py
+++ b/solution.py
@@ -454,6 +454,29 @@
             send("rows", r, glp.at[lax.rem(r + k, N)], grs.at[0, r], 2, k).start()
 
     plane.tasks = plane.tasks + [finish_fact, left_gram]
+    plane.tick()
+    plane.tick()
+    pending, groups = [], []
+
+    def solve(sources):
+        pending.extend(sources)
+        groups.append(len(sources))
+        if len(groups) < 4:
+            return
+        if len(groups) == 4:
+
+            @pl.loop(1, N)
+            def _(k):
+                source = lax.rem(c + N - k, N)
+                arrival("ckpt", fall.at[rows64(source)], 1, source)
+
+        for dx, dy in pending:
+            o = plane.place(0, dx, dy)
+            block = rows64(xor(o, c))
+            rall[block, :] = jnp.dot(
+                fall[block, :RANK], raw[o], preferred_element_type=F32
+            ).astype(BF)
+        pending.clear()
 
     def landed(h):
         @pl.when(r != 0)
@@ -464,22 +487,9 @@
         lambda h, o: raw.at[o, pl.ds(32 * h, 32)],
         lambda h, o, q: raw.at[o, pl.ds(32 * h + 16 * q, 16)],
         192,
-        lambda sources: None,
+        solve,
         landed,
     )
-
-    @pl.loop(1, N)
-    def _(k):
-        source = lax.rem(c + N - k, N)
-        arrival("ckpt", fall.at[rows64(source)], 1, source)
-
-    @pl.loop(0, N)
-    def _(o):
-        e = xor(o, c)
-        rall[rows64(e), :] = jnp.dot(
-            fall[rows64(e), :RANK], raw[o], preferred_element_type=F32
-        ).astype(BF)
-
     first_row, pair = tile_of(r)
     pair_rows = pl.ds(pl.multiple_of(lax.div(r, 2) * 128, 128), 128)
     half_rows = pl.ds(pl.multiple_of(first_row, 512), 512)

time: 186 us -> 182 us (0.978)
  Pallas kernels: 184 us -> 179 us
    pallas_call x1, Pallas kernels: 184 us -> 179 us  [body(): pl.pallas_call(merge_kernel, out_shape=jax.ShapeDtypeStruct((ROWS, COLS),...]
where the time goes in v6:
time: 182 us; the launch traced here: 181 us
  Pallas kernels  179 us (98%)
  local copies, waits for them, and re-layouts  1.82 us (1%)
    pallas_call x1, Pallas kernels, body(): pl.pallas_call(merge_kernel, out_shape=jax.ShapeDtypeStruct((ROWS, COLS),...  179 us

profile of v6, /device:TPU:8, one launch (start us, length us, event | category | flops | bytes accessed | tf_op | source)
XLA Modules:
  0.0 181.3 jit_solution(9867159272090707629)
XLA Ops:
  0.0 179.5 %merge.1 = bf16[256,896]{1,0:T(8,128)(2,1)} custom-call(bf16[256,14336]{1,0:T(8,128)(2,1)} %bitcast.4, bf16[64,896]{1,0:T(8,128)(2,1)} %bitcast.5, s32[16]{0:T(128)} %order.1), custom_call_target="tpu_custom_call" | custom-call | tf_op jit(solution)/shard_map/merge/pallas_call | solution.py:630
  179.5 1.8 %copy.5 = bf16[256,896]{1,0:T(8,128)(2,1)} copy(bf16[256,896]{1,0:T(8,128)(2,1)} %merge.1) | data formatting | bytes 917504
